TPU v7x, 768 devices: a whole 4x8x12 slice. The times are simulated.
768 devices in a mesh: band: 16 (over z_hi, x, core), member: 48 (over z_lo, y).
Axes of the slice: x: 4, y: 8, z: 12 (z_hi: 2, z_lo: 6; z = z_hi * 6 + z_lo), core: 2. Of those that a mesh axis runs over, the one named last changes fastest.
Arguments:
- checkpoints: float32 [48, 3, 4, 128, 512], P('member', None, None, 'band'), may hold values from -3 to 3
- ckpt_index: int32 [2], replicated, may hold values from 0 to 47, as said below
- innovations: float32 [2, 3, 4, 128, 512], P(None, None, None, 'band'), may hold values from -6 to 6
- seeds: int32 [48], P('member'), may hold values from 0 to 511
Outputs:
- adjoint: float32 [48, 3, 4, 128, 512], P('member', None, None, 'band')
Inputs may be any that keep to these rules, and one draw needn't show every extreme that they name: `ckpt_index`: distinct slot indices of checkpoints, one for each interval; one of them is the last slot, 47. `seeds`: a longitude shift in cells.
All inputs are finite; a program needn't handle non-finite values.
Results may differ from a plain program's by a relative error of at most 0.0003.
Values sent between devices are 32-bit elements; how exact they have to be, the bound alone decides.
A program may use at most 32 MiB of HBM per device.

v0:
```python
import jax
import jax.numpy as jnp
from jax import lax
from jax.sharding import PartitionSpec as P

INTERVALS = 2
STEPS = 2


TIME_STEP = 0.2
VISCOSITY_BASE = 0.2


def with_halo(array, sides, width):
    for axis, dim in sides:
        count, length = (lax.axis_size(axis), array.shape[dim])
        up = [(i, (i + 1) % count) for i in range(count - 1)]
        down = [(j, i) for i, j in up]
        last = lax.slice_in_dim(array, length - width, length, axis=dim)
        initial = lax.slice_in_dim(array, 0, width, axis=dim)
        before = lax.ppermute(last, axis, up)
        after = lax.ppermute(initial, axis, down)
        array = jnp.concatenate([before, array, after], axis=dim)
    return array


def broadcast(value, axis, source):
    kept = jnp.where(lax.axis_index(axis) == source, value, 0).astype(value.dtype)
    return lax.psum(kept, axis)


def zonal_diff(field_in):
    return 0.5 * (jnp.roll(field_in, -1, -1) - jnp.roll(field_in, 1, -1))


def advance(state):
    east_wind, north_wind, height = (state[0], state[1], state[2])
    new_east = east_wind - TIME_STEP * (east_wind * zonal_diff(east_wind) + zonal_diff(height))
    new_north = north_wind - TIME_STEP * (east_wind * zonal_diff(north_wind))
    new_height = height - TIME_STEP * (east_wind * zonal_diff(height) + zonal_diff(east_wind))
    return jnp.stack([new_east, new_north, new_height])


def trajectory(initial):
    states = [initial]
    states.append(advance(states[-1]))
    return states


def interior(field_in):
    return field_in[..., 1:-1, :]


def merid_diff(field_in):
    return 0.5 * (field_in[..., 2:, :] - field_in[..., :-2, :])


def laplacian(field_in):
    centre = interior(field_in)
    return (
        field_in[..., 2:, :]
        + field_in[..., :-2, :]
        + jnp.roll(centre, -1, -1)
        + jnp.roll(centre, 1, -1)
        - 4.0 * centre
    )


def tendency(state_ext, adjoint_ext):
    east_wind = interior(state_ext[0])
    north_wind = state_ext[1]
    layer_depth = jnp.exp(0.25 * interior(state_ext[2]))
    viscosity = VISCOSITY_BASE * (1.0 + 0.5 * jnp.tanh(state_ext[2]))
    east_part = adjoint_ext[..., 0, :, :, :]
    north_part = adjoint_ext[..., 1, :, :, :]
    height_part = adjoint_ext[..., 2, :, :, :]
    tend_east = (
        zonal_diff(east_wind * interior(east_part))
        + merid_diff(north_wind * east_part)
        + layer_depth * zonal_diff(interior(height_part))
        + laplacian(viscosity * east_part)
    )
    tend_north = (
        zonal_diff(east_wind * interior(north_part))
        + merid_diff(north_wind * north_part)
        + layer_depth * merid_diff(height_part)
        + laplacian(viscosity * north_part)
    )
    tend_height = (
        zonal_diff(east_wind * interior(height_part))
        + merid_diff(north_wind * height_part)
        + zonal_diff(interior(east_part))
        + merid_diff(north_part)
        + laplacian(viscosity * height_part)
    )
    return jnp.stack([tend_east, tend_north, tend_height], axis=-4)


def shift_lon(field_in, amount):
    lon_cells = field_in.shape[-1]
    joined = jnp.concatenate([field_in, field_in], axis=-1)
    return lax.dynamic_slice_in_dim(joined, lon_cells - amount, lon_cells, field_in.ndim - 1)


def on_device(checkpoints, ckpt_index, innovations, seeds):
    own_slot = checkpoints[0]
    slot_ext = with_halo(own_slot, (("band", 2),), 1)
    own_states = jnp.stack(trajectory(slot_ext))
    adjoint = jnp.zeros((seeds.shape[0],) + innovations.shape[1:], jnp.float32)
    for interval in reversed(range(INTERVALS)):
        root_group = ckpt_index[interval]
        received = broadcast(own_states, "member", root_group)
        tiles = [received[step] for step in range(STEPS)]
        current = innovations[interval]

        def member_forcing(member_seed):
            return shift_lon(current, member_seed)

        adjoint = adjoint + jax.vmap(member_forcing)(seeds)
        for step in reversed(range(STEPS)):
            adjoint_ext = with_halo(adjoint, (("band", 3),), 1)
            adjoint = adjoint + TIME_STEP * tendency(tiles[step], adjoint_ext)
    return adjoint


def solution(mesh):
    return jax.shard_map(
        on_device,
        mesh=mesh,
        in_specs=(
            P("member", None, None, "band", None),
            P(),
            P(None, None, None, "band", None),
            P("member"),
        ),
        out_specs=P("member", None, None, "band", None),
        check_vma=False,
    )
```

profile of v0, /device:TPU:7, one launch (start us, length us, event | category | flops | bytes accessed | tf_op | source)
XLA Modules:
  0.0 697.4 jit_solution(13068208754894637577)
XLA Ops:
  6.5 1.1 fusion.158
  7.6 2.6 collective-permute-start.1
  10.2 14.7 %collective-permute-start = (f32[3,4,1,512]{3,2,1,0:T(1,128)S(1)}, f32[3,4,1,512]{3,2,1,0:T(1,128)S(1)}, u32[]{:S(2)}, u32[]{:S(2)}) collective-permute-start(f32[3,4,1,512]{3,2,1,0:T(1,128)S(1)} %get-tuple-element.92), channel_id=1, source_target_pairs={{0,48},{48,96},{96,144},{144,192},{192,240},{240,288},{288,336},{3... | collective-permute-start | bytes 73736 | tf_op jit(solution)/shard_map/ppermute | solution.py:21
  25.5 1.1 slice_bitcast_fusion.1
  26.6 0.2 fusion.6
  26.8 1.9 collective-permute-start.3
  28.8 12.1 %collective-permute-start.2 = (f32[1,3,4,1,512]{4,3,2,1,0:T(1,128)S(1)}, f32[1,3,4,1,512]{4,3,2,1,0:T(1,128)S(1)}, u32[]{:S(2)}, u32[]{:S(2)}) collective-permute-start(f32[1,3,4,1,512]{4,3,2,1,0:T(1,128)S(1)} %get-tuple-element.90), channel_id=1, source_target_pairs={{0,48},{48,96},{96,144},{144,192},{192,240},{240,288},{288,336},{3... | collective-permute-start | bytes 73736 | tf_op jit(solution)/shard_map/ppermute | solution.py:21
  40.8 0.7 fusion.215
  43.5 0.2 multiply_subtract_fusion.1
  43.7 1.4 fusion
  45.6 558.5 %all-reduce.3.cloned.1.call-done = (f32[2,3,4,10,512]{4,3,2,1,0:T(8,128)}, f32[2,3,4,10,512]{4,3,2,1,0:T(8,128)}) async-done(((f32[2,3,4,10,512]{4,3,2,1,0:T(8,128)}, f32[2,3,4,10,512]{4,3,2,1,0:T(8,128)}), (f32[2,3,4,10,512]{4,3,2,1,0:T(8,128)}, f32[2,3,4,10,512]{4,3,2,1,0:T(8,128)})) %all-reduce.3.cloned.1.call-update) | async-done | bytes 983056 | tf_op jit(solution)/shard_map/psum | solution.py:29
  604.1 1.1 fusion.19
  606.9 0.2 fusion.7
  607.1 36.7 %collective-permute-start.5 = (f32[1,3,4,1,512]{4,3,2,1,0:T(1,128)S(1)}, f32[1,3,4,1,512]{4,3,2,1,0:T(1,128)S(1)}, u32[]{:S(2)}, u32[]{:S(2)}) collective-permute-start(f32[1,3,4,1,512]{4,3,2,1,0:T(1,128)S(1)} %get-tuple-element.89), channel_id=1, source_target_pairs={{48,0},{96,48},{144,96},{192,144},{240,192},{288,240},{336,288},{3... | collective-permute-start | bytes 73736 | tf_op jit(solution)/shard_map/ppermute | solution.py:22
  643.8 7.7 %collective-permute-start.4 = (f32[1,3,4,1,512]{4,3,2,1,0:T(1,128)S(1)}, f32[1,3,4,1,512]{4,3,2,1,0:T(1,128)S(1)}, u32[]{:S(2)}, u32[]{:S(2)}) collective-permute-start(f32[1,3,4,1,512]{4,3,2,1,0:T(1,128)S(1)} %get-tuple-element.88), channel_id=1, source_target_pairs={{0,48},{48,96},{96,144},{144,192},{192,240},{240,288},{288,336},{3... | collective-permute-start | bytes 73736 | tf_op jit(solution)/shard_map/ppermute | solution.py:21
  651.5 0.9 collective-permute-done.4
  654.4 0.3 fusion.4
  654.8 1.9 collective-permute-start.7
  656.7 12.6 %collective-permute-start.6 = (f32[1,3,4,1,512]{4,3,2,1,0:T(1,128)S(1)}, f32[1,3,4,1,512]{4,3,2,1,0:T(1,128)S(1)}, u32[]{:S(2)}, u32[]{:S(2)}) collective-permute-start(f32[1,3,4,1,512]{4,3,2,1,0:T(1,128)S(1)} %get-tuple-element.86), channel_id=1, source_target_pairs={{0,48},{48,96},{96,144},{144,192},{192,240},{240,288},{288,336},{3... | collective-permute-start | bytes 73736 | tf_op jit(solution)/shard_map/ppermute | solution.py:21
  669.4 0.9 collective-permute-done.6
  672.3 1.9 collective-permute-start.9
  674.3 12.6 %collective-permute-start.8 = (f32[1,3,4,1,512]{4,3,2,1,0:T(1,128)S(1)}, f32[1,3,4,1,512]{4,3,2,1,0:T(1,128)S(1)}, u32[]{:S(2)}, u32[]{:S(2)}) collective-permute-start(f32[1,3,4,1,512]{4,3,2,1,0:T(1,128)S(1)} %get-tuple-element.84), channel_id=1, source_target_pairs={{0,48},{48,96},{96,144},{144,192},{192,240},{240,288},{288,336},{3... | collective-permute-start | bytes 73736 | tf_op jit(solution)/shard_map/ppermute | solution.py:21
  686.9 0.9 collective-permute-done.8
  689.8 0.7 fusion.10
  (123 shorter events, 8.6 us)
Async XLA Ops:
  6.5 597.6 %all-reduce.3.cloned.1.call-start = ((), (), s32[]{:S(2)}) async-start(), calls=%async_computation | async-start | bytes 3145728 | tf_op jit(solution)/shard_map/psum | solution.py:29
  7.6 35.3 %collective-permute-start.1 = (f32[3,4,1,512]{3,2,1,0:T(1,128)S(1)}, f32[3,4,1,512]{3,2,1,0:T(1,128)S(1)}, u32[]{:S(2)}, u32[]{:S(2)}) collective-permute-start(f32[3,4,1,512]{3,2,1,0:T(1,128)S(1)} %get-tuple-element.93), channel_id=1, source_target_pairs={{48,0},{96,48},{144,96},{192,144},{240,192},{288,240},{336,288},{3... | collective-permute-start | bytes 73736 | tf_op jit(solution)/shard_map/ppermute | solution.py:22
  10.2 32.7 %collective-permute-start = (f32[3,4,1,512]{3,2,1,0:T(1,128)S(1)}, f32[3,4,1,512]{3,2,1,0:T(1,128)S(1)}, u32[]{:S(2)}, u32[]{:S(2)}) collective-permute-start(f32[3,4,1,512]{3,2,1,0:T(1,128)S(1)} %get-tuple-element.92), channel_id=1, source_target_pairs={{0,48},{48,96},{96,144},{144,192},{192,240},{240,288},{288,336},{3... | collective-permute-start | bytes 73736 | tf_op jit(solution)/shard_map/ppermute | solution.py:21
  26.6 16.3 %copy-start.2 = (f32[1,3,4,8,512]{4,3,2,1,0:T(8,128)S(1)}, f32[1,3,4,8,512]{4,3,2,1,0:T(8,128)}, u32[]{:S(2)}) copy-start(f32[1,3,4,8,512]{4,3,2,1,0:T(8,128)} %param.4) | copy-start | bytes 589828
  26.8 14.0 %copy-start.3 = (s32[2]{0:T(128)S(1)}, s32[2]{0:T(128)}, u32[]{:S(2)}) copy-start(s32[2]{0:T(128)} %param.5) | copy-start | bytes 28
  26.8 18.3 %collective-permute-start.3 = (f32[1,3,4,1,512]{4,3,2,1,0:T(1,128)S(1)}, f32[1,3,4,1,512]{4,3,2,1,0:T(1,128)S(1)}, u32[]{:S(2)}, u32[]{:S(2)}) collective-permute-start(f32[1,3,4,1,512]{4,3,2,1,0:T(1,128)S(1)} %get-tuple-element.91), channel_id=1, source_target_pairs={{48,0},{96,48},{144,96},{192,144},{240,192},{288,240},{336,288},{3... | collective-permute-start | bytes 73736 | tf_op jit(solution)/shard_map/ppermute | solution.py:22
  28.8 16.4 %collective-permute-start.2 = (f32[1,3,4,1,512]{4,3,2,1,0:T(1,128)S(1)}, f32[1,3,4,1,512]{4,3,2,1,0:T(1,128)S(1)}, u32[]{:S(2)}, u32[]{:S(2)}) collective-permute-start(f32[1,3,4,1,512]{4,3,2,1,0:T(1,128)S(1)} %get-tuple-element.90), channel_id=1, source_target_pairs={{0,48},{48,96},{96,144},{144,192},{192,240},{240,288},{288,336},{3... | collective-permute-start | bytes 73736 | tf_op jit(solution)/shard_map/ppermute | solution.py:21
  604.1 1.3 copy-start.1
  607.1 44.4 %collective-permute-start.5 = (f32[1,3,4,1,512]{4,3,2,1,0:T(1,128)S(1)}, f32[1,3,4,1,512]{4,3,2,1,0:T(1,128)S(1)}, u32[]{:S(2)}, u32[]{:S(2)}) collective-permute-start(f32[1,3,4,1,512]{4,3,2,1,0:T(1,128)S(1)} %get-tuple-element.89), channel_id=1, source_target_pairs={{48,0},{96,48},{144,96},{192,144},{240,192},{288,240},{336,288},{3... | collective-permute-start | bytes 73736 | tf_op jit(solution)/shard_map/ppermute | solution.py:22
  643.8 8.6 %collective-permute-start.4 = (f32[1,3,4,1,512]{4,3,2,1,0:T(1,128)S(1)}, f32[1,3,4,1,512]{4,3,2,1,0:T(1,128)S(1)}, u32[]{:S(2)}, u32[]{:S(2)}) collective-permute-start(f32[1,3,4,1,512]{4,3,2,1,0:T(1,128)S(1)} %get-tuple-element.88), channel_id=1, source_target_pairs={{0,48},{48,96},{96,144},{144,192},{192,240},{240,288},{288,336},{3... | collective-permute-start | bytes 73736 | tf_op jit(solution)/shard_map/ppermute | solution.py:21
  654.3 15.1 %copy-start = (f32[2,3,4,10,512]{4,3,2,1,0:T(8,128)S(1)}, f32[2,3,4,10,512]{4,3,2,1,0:T(8,128)}, u32[]{:S(2)}) copy-start(f32[2,3,4,10,512]{4,3,2,1,0:T(8,128)} %get-tuple-element.28) | copy-start | bytes 1474564
  654.8 14.6 %collective-permute-start.7 = (f32[1,3,4,1,512]{4,3,2,1,0:T(1,128)S(1)}, f32[1,3,4,1,512]{4,3,2,1,0:T(1,128)S(1)}, u32[]{:S(2)}, u32[]{:S(2)}) collective-permute-start(f32[1,3,4,1,512]{4,3,2,1,0:T(1,128)S(1)} %get-tuple-element.87), channel_id=1, source_target_pairs={{48,0},{96,48},{144,96},{192,144},{240,192},{288,240},{336,288},{3... | collective-permute-start | bytes 73736 | tf_op jit(solution)/shard_map/ppermute | solution.py:22
  656.7 13.6 %collective-permute-start.6 = (f32[1,3,4,1,512]{4,3,2,1,0:T(1,128)S(1)}, f32[1,3,4,1,512]{4,3,2,1,0:T(1,128)S(1)}, u32[]{:S(2)}, u32[]{:S(2)}) collective-permute-start(f32[1,3,4,1,512]{4,3,2,1,0:T(1,128)S(1)} %get-tuple-element.86), channel_id=1, source_target_pairs={{0,48},{48,96},{96,144},{144,192},{192,240},{240,288},{288,336},{3... | collective-permute-start | bytes 73736 | tf_op jit(solution)/shard_map/ppermute | solution.py:21
  672.3 14.6 %collective-permute-start.9 = (f32[1,3,4,1,512]{4,3,2,1,0:T(1,128)S(1)}, f32[1,3,4,1,512]{4,3,2,1,0:T(1,128)S(1)}, u32[]{:S(2)}, u32[]{:S(2)}) collective-permute-start(f32[1,3,4,1,512]{4,3,2,1,0:T(1,128)S(1)} %get-tuple-element.85), channel_id=1, source_target_pairs={{48,0},{96,48},{144,96},{192,144},{240,192},{288,240},{336,288},{3... | collective-permute-start | bytes 73736 | tf_op jit(solution)/shard_map/ppermute | solution.py:22
  674.3 13.6 %collective-permute-start.8 = (f32[1,3,4,1,512]{4,3,2,1,0:T(1,128)S(1)}, f32[1,3,4,1,512]{4,3,2,1,0:T(1,128)S(1)}, u32[]{:S(2)}, u32[]{:S(2)}) collective-permute-start(f32[1,3,4,1,512]{4,3,2,1,0:T(1,128)S(1)} %get-tuple-element.84), channel_id=1, source_target_pairs={{0,48},{48,96},{96,144},{144,192},{192,240},{240,288},{288,336},{3... | collective-permute-start | bytes 73736 | tf_op jit(solution)/shard_map/ppermute | solution.py:21
Sparse Core Ops, SparseCore 0:
  45.3 558.7 all-reduce.2
where the time goes:
time: 698 us; the launch traced here: 697 us
  waiting for transfers between devices  561 us (80%)
  starting transfers between devices  105 us (15%)
  between operations  16 us (2%)
  local copies, waits for them, and re-layouts  8.75 us (1%)
    psum x1, waiting for transfers between devices, broadcast(): return lax.psum(kept, axis)  558 us
    ppermute x5, starting transfers between devices, with_halo(): before = lax.ppermute(last, axis, up)  59.7 us
    ppermute x5, starting transfers between devices, with_halo(): after = lax.ppermute(initial, axis, down)  45.1 us
  transfers between devices with their start and end apart: 11, of which 4 were waited for; matrix products, arithmetic and copies ran while one was open for 1% of the time, Pallas kernels for 0%

commit v1 on v0

v1 whole, which is shorter than its diff:
```python
import functools

import jax
import jax.numpy as jnp
from jax import lax
from jax.experimental import pallas as pl
from jax.experimental.pallas import tpu as pltpu
from jax.sharding import PartitionSpec as P

NY = 8
NZ = 6
NBAND = 16
LEV = 4
PLANES = 3 * LEV
HALF = PLANES // 2
ROWS = 8
LON = 512
LAST_SLOT = 47
MESH = pl.DeviceIdType.MESH


def next_lon(x):
    return pltpu.roll(x, LON - 1, 1)


def prev_lon(x):
    return pltpu.roll(x, 1, 1)


def next_row(x):
    return pltpu.roll(x, 2 * ROWS - 1, 0)


def prev_row(x):
    return pltpu.roll(x, 1, 0)


def advance(east, north, height):
    diff_east = 0.1 * (next_lon(east) - prev_lon(east))
    diff_north = 0.1 * (next_lon(north) - prev_lon(north))
    diff_height = 0.1 * (next_lon(height) - prev_lon(height))
    return (
        east - (east * diff_east + diff_height),
        north - east * diff_north,
        height - (east * diff_height + diff_east),
    )


def adjoint_step(state, adjoint, keep):
    east, north, height = state
    a, b, c = adjoint
    depth = 0.1 * jnp.exp(0.25 * height)
    visc = 0.04 + 0.02 * jnp.tanh(height)
    east, north = 0.1 * east, 0.1 * north
    c_next, c_prev = visc + east, visc - east
    r_next, r_prev = visc + north, visc - north
    middle = 1.0 - 4.0 * visc

    def spread(f, zonal=None, merid=None):
        if zonal is None:
            zonal = merid = 0.0
        return (
            middle * f
            + next_lon(c_next * f + zonal)
            + prev_lon(c_prev * f - zonal)
            + next_row(r_next * f + merid)
            + prev_row(r_prev * f - merid)
        )

    new_a = spread(a) + depth * (next_lon(c) - prev_lon(c))
    new_b = spread(b) + depth * (next_row(c) - prev_row(c))
    new_c = spread(c, 0.1 * a, 0.1 * b)
    return tuple(jnp.where(keep, f, 0.0) for f in (new_a, new_b, new_c))


def kernel(
    index_ref, seed_ref, ckpt, innov, out,
    row_in, col_in, last_in, piece, own, edge, force, force_edge,
    row_sem, col_sem, last_sem, gather_sem, place_sem, edge_sem, far_sem, force_sem, load_sem,
):
    band = lax.axis_index("band")
    member = lax.axis_index("member")
    y, z = lax.rem(member, NY), member // NY
    has_up = band < NBAND - 1
    has_down = band > 0
    up, down = {"band": band + 1}, {"band": band - 1}

    def y_peer(step):
        return lax.rem(y + step, NY)

    def z_peer(step):
        return lax.rem(z + step, NZ)

    def at_y(peer):
        return {"member": z * NY + peer}

    def at_z(peer):
        return {"member": peer * NY + y}

    def part(peer):
        planes = pl.ds(HALF * (peer // 4), HALF)
        lanes = pl.ds(pl.multiple_of(128 * lax.rem(peer, 4), 128), 128)
        return planes, slice(None), lanes

    def send(src, dst, sems, device):
        return pltpu.make_async_remote_copy(
            src_ref=src, dst_ref=dst, send_sem=sems.at[0], recv_sem=sems.at[1],
            device_id=device, device_id_type=MESH,
        )

    load = pltpu.make_async_copy(innov, force, load_sem)
    load.start()
    edge[...] = jnp.zeros_like(edge)
    force_edge[...] = jnp.zeros_like(force_edge)

    barrier = pltpu.get_barrier_semaphore()
    for step in range(1, NY):
        pl.semaphore_signal(barrier, inc=1, device_id=at_y(y_peer(step)), device_id_type=MESH)
    for step in range(1, NZ):
        pl.semaphore_signal(barrier, inc=1, device_id=at_z(z_peer(step)), device_id_type=MESH)

    @pl.when(has_up)
    def _():
        pl.semaphore_signal(barrier, inc=1, device_id=up, device_id_type=MESH)

    @pl.when(has_down)
    def _():
        pl.semaphore_signal(barrier, inc=1, device_id=down, device_id_type=MESH)

    @pl.when(jnp.logical_and(has_up, has_down))
    def _():
        pl.semaphore_wait(barrier, NY + NZ)

    @pl.when(jnp.logical_not(jnp.logical_and(has_up, has_down)))
    def _():
        pl.semaphore_wait(barrier, NY + NZ - 1)

    for step in range(1, NY):
        peer = y_peer(step)
        send(ckpt.at[part(peer)], row_in.at[y], row_sem, at_y(peer)).start()
    mine = pltpu.make_async_copy(ckpt.at[part(y)], row_in.at[y], place_sem.at[0])
    mine.start()

    def force_up(k):
        rows = (k, slice(None), slice(4, 8))
        return send(innov.at[rows], force_edge.at[rows], force_sem.at[k, 0], up)

    def force_down(k):
        rows = (k, slice(None), slice(0, 4))
        return send(innov.at[rows], force_edge.at[rows], force_sem.at[k, 1], down)

    for k in (1, 0):
        @pl.when(has_up)
        def _():
            force_up(k).start()

        @pl.when(has_down)
        def _():
            force_down(k).start()

    load.wait()
    seed = seed_ref[0]
    for k in range(2):
        for plane in range(PLANES):
            force[k, plane] = pltpu.roll(force[k, plane], seed, 1)

    mine.wait()
    send(row_in.at[pl.ds(0, NY - 1)], row_in.at[pl.ds(0, NY - 1)], row_sem, at_y(y_peer(1))).wait()

    other = jnp.where(index_ref[0] == LAST_SLOT, index_ref[1], index_ref[0])
    col_in[z] = row_in[lax.rem(other, NY)]
    for step in range(1, NZ):
        send(col_in.at[z], col_in.at[z], col_sem, at_z(z_peer(step))).start()

    @pl.when(z == NZ - 1)
    def _():
        last_in[...] = row_in[NY - 1]
        for step in range(1, NZ):
            send(last_in, last_in, last_sem, at_z(z_peer(step))).start()

    send(col_in.at[pl.ds(0, NZ - 1)], col_in.at[pl.ds(0, NZ - 1)], col_sem, at_z(z_peer(1))).wait()

    @pl.when(z == NZ - 1)
    def _():
        send(col_in.at[pl.ds(0, NZ - 1)], col_in.at[pl.ds(0, NZ - 1)], last_sem, at_z(z_peer(1))).wait_send()

    @pl.when(z < NZ - 1)
    def _():
        send(last_in, last_in, last_sem, at_z(z_peer(1))).wait_recv()

    from_other = col_in[other // NY]
    from_last = last_in[...]
    for k in (1, 0):
        piece[k] = jnp.where(index_ref[k] == LAST_SLOT, from_last, from_other)
    places = []
    for k in (1, 0):
        for step in range(1, NY):
            send(piece.at[k], own.at[(k,) + part(y)], gather_sem.at[k], at_y(y_peer(step))).start()
        places.append(pltpu.make_async_copy(piece.at[k], own.at[(k,) + part(y)], place_sem.at[1 + k]))
        places[-1].start()

    def edge_up(k):
        rows = (k, slice(None), slice(4, 8))
        return send(own.at[rows], edge.at[rows], edge_sem.at[k, 0], up)

    def edge_down(k):
        rows = (k, slice(None), slice(0, 4))
        return send(own.at[rows], edge.at[rows], edge_sem.at[k, 1], down)

    for k in (1, 0):
        @pl.when(has_up)
        def _():
            force_up(k).wait_send()
            force_down(k).wait_recv()

        @pl.when(has_down)
        def _():
            force_down(k).wait_send()
            force_up(k).wait_recv()

        for plane in range(PLANES):
            force_edge[k, plane] = pltpu.roll(force_edge[k, plane], seed, 1)

    for place, k in zip(places, (1, 0)):
        place.wait()
        send(row_in.at[pl.ds(0, NY - 1)], row_in.at[pl.ds(0, NY - 1)], gather_sem.at[k], at_y(y_peer(1))).wait()

        @pl.when(has_up)
        def _():
            edge_up(k).start()

        @pl.when(has_down)
        def _():
            edge_down(k).start()

    row = lax.broadcasted_iota(jnp.int32, (2 * ROWS, LON), 0)
    outside = jnp.logical_or(
        jnp.logical_and(band == NBAND - 1, jnp.logical_and(row >= 8, row < 12)),
        jnp.logical_and(band == 0, row >= 12),
    )
    keep = jnp.logical_not(outside)

    adjoint = [None] * LEV
    for k in (1, 0):
        @pl.when(has_up)
        def _():
            edge_up(k).wait_send()
            edge_down(k).wait_recv()

        @pl.when(has_down)
        def _():
            edge_down(k).wait_send()
            edge_up(k).wait_recv()

        for lev in range(LEV):
            def both(inner, outer):
                return tuple(
                    jnp.concatenate([inner[k, comp * LEV + lev], outer[k, comp * LEV + lev]], axis=0)
                    for comp in range(3)
                )

            forcing = both(force, force_edge)
            if adjoint[lev] is None:
                field = forcing
            else:
                field = tuple(f + g for f, g in zip(adjoint[lev], forcing))
            first = both(own, edge)
            field = adjoint_step(advance(*first), field, keep)
            field = adjoint_step(first, field, keep)
            if k == 1:
                adjoint[lev] = field
            else:
                for comp in range(3):
                    out[comp * LEV + lev] = field[comp][:ROWS]


def on_device(checkpoints, ckpt_index, innovations, seeds):
    slot = checkpoints.reshape(PLANES, ROWS, LON)
    current = innovations.reshape(2, PLANES, ROWS, LON)
    any_space = pl.BlockSpec(memory_space=pl.ANY)
    smem = pl.BlockSpec(memory_space=pltpu.SMEM)
    field = (2, PLANES, ROWS, LON)
    dma = pltpu.SemaphoreType.DMA
    result = pl.pallas_call(
        kernel,
        out_shape=jax.ShapeDtypeStruct((PLANES, ROWS, LON), jnp.float32),
        in_specs=[smem, smem, any_space, any_space],
        out_specs=pl.BlockSpec(memory_space=pltpu.VMEM),
        scratch_shapes=[
            pltpu.VMEM((NY, HALF, ROWS, 128), jnp.float32),
            pltpu.VMEM((NZ, HALF, ROWS, 128), jnp.float32),
            pltpu.VMEM((HALF, ROWS, 128), jnp.float32),
            pltpu.VMEM((2, HALF, ROWS, 128), jnp.float32),
            pltpu.VMEM(field, jnp.float32),
            pltpu.VMEM(field, jnp.float32),
            pltpu.VMEM(field, jnp.float32),
            pltpu.VMEM(field, jnp.float32),
            dma((2,)),
            dma((2,)),
            dma((2,)),
            dma((2, 2)),
            dma((3,)),
            dma((2, 2, 2)),
            dma((2,)),
            dma((2, 2, 2)),
            dma,
        ],
        compiler_params=pltpu.CompilerParams(
            collective_id=0, has_side_effects=True, vmem_limit_bytes=32 * 2**20
        ),
        name="ensemble_adjoint",
    )(ckpt_index, seeds, slot, current)
    return result.reshape(1, 3, LEV, ROWS, LON)


def solution(mesh):
    return jax.shard_map(
        on_device,
        mesh=mesh,
        in_specs=(
            P("member", None, None, "band", None),
            P(),
            P(None, None, None, "band", None),
            P("member"),
        ),
        out_specs=P("member", None, None, "band", None),
        check_vma=False,
    )
```

time: 698 us -> 56.9 us (0.08)
  the two profiles are of different devices: /device:TPU:7 before, /device:TPU:71 now
where the time goes in v1:
time: 56.9 us; the launch traced here: 56.7 us
  Pallas kernels  52.8 us (93%)
  local copies, waits for them, and re-layouts  3.25 us (6%)
  between operations  0.67 us (1%)
    pallas_call x1, Pallas kernels, on_device(): pl.pallas_call(kernel, out_shape=jax.ShapeDtypeStruct((PLANES, ROWS, LON)...  52.8 us
    unnamed x7, local copies, waits for them, and re-layouts  3.25 us

profile of v1, /device:TPU:71, one launch (start us, length us, event | category | flops | bytes accessed | tf_op | source)
XLA Modules:
  0.0 56.7 jit_solution(2816957888282664913)
XLA Ops:
  0.7 0.0 copy-start.2
  0.7 0.6 %copy-done.2 = s32[2]{0:T(128)S(1)} copy-done((s32[2]{0:T(128)S(1)}, s32[2]{0:T(128)}, u32[]{:S(2)}) %copy-start.2) | copy-done | bytes 32
  1.3 0.0 copy-start
  1.3 1.0 %copy-done = f32[2,3,4,8,512]{4,3,2,1,0:T(8,128)S(1)} copy-done((f32[2,3,4,8,512]{4,3,2,1,0:T(8,128)S(1)}, f32[2,3,4,8,512]{4,3,2,1,0:T(8,128)}, u32[]{:S(2)}) %copy-start) | copy-done | bytes 393240
  2.3 0.0 copy-start.1
  2.3 0.9 %copy-done.1 = f32[1,3,4,8,512]{4,3,2,1,0:T(8,128)S(1)} copy-done((f32[1,3,4,8,512]{4,3,2,1,0:T(8,128)S(1)}, f32[1,3,4,8,512]{4,3,2,1,0:T(8,128)}, u32[]{:S(2)}) %copy-start.1) | copy-done | bytes 196632
  3.2 52.8 %ensemble_adjoint.1 = f32[12,8,512]{2,1,0:T(8,128)S(1)} custom-call(s32[2]{0:T(128)S(1)} %copy-done.2, s32[1]{0:T(128)S(6)} %copy.6.seed_ref, f32[12,8,512]{2,1,0:T(8,128)S(1)} %bitcast.5, f32[2,12,8,512]{3,2,1,0:T(8,128)S(1)} %bitcast.4), custom_call_target="tpu_custom_call" | custom-call | tf_op jit(solution)/shard_map/ensemble_adjoint/pallas_call | solution.py:284
  56.1 0.7 %copy.7 = f32[1,3,4,8,512]{4,3,2,1,0:T(8,128)} copy(f32[1,3,4,8,512]{4,3,2,1,0:T(8,128)S(1)} %bitcast.3) | data formatting | bytes 393216
Async XLA Ops:
  0.7 0.7 %copy-start.2 = (s32[2]{0:T(128)S(1)}, s32[2]{0:T(128)}, u32[]{:S(2)}) copy-start(s32[2]{0:T(128)} %index_ref.1) | copy-start | bytes 28
  1.3 1.0 %copy-start = (f32[2,3,4,8,512]{4,3,2,1,0:T(8,128)S(1)}, f32[2,3,4,8,512]{4,3,2,1,0:T(8,128)}, u32[]{:S(2)}) copy-start(f32[2,3,4,8,512]{4,3,2,1,0:T(8,128)} %param.6) | copy-start | bytes 1179652
  2.3 0.9 %copy-start.1 = (f32[1,3,4,8,512]{4,3,2,1,0:T(8,128)S(1)}, f32[1,3,4,8,512]{4,3,2,1,0:T(8,128)}, u32[]{:S(2)}) copy-start(f32[1,3,4,8,512]{4,3,2,1,0:T(8,128)} %param.4) | copy-start | bytes 589828

commit v2 on v1

v2 whole, which is shorter than its diff:
```python
import jax
import jax.numpy as jnp
from jax import lax
from jax.experimental import pallas as pl
from jax.experimental.pallas import tpu as pltpu
from jax.sharding import PartitionSpec as P

NY = 8
NZ = 6
NBAND = 16
LOW_FAR, HIGH_FAR = NBAND // 2 - 1, NBAND // 2
LEV = 4
PLANES = 3 * LEV
HALF = PLANES // 2
ROWS = 8
LON = 512
LAST_SLOT = NY * NZ - 1
EDGE = {1: 4, 0: 2}
MESH = pl.DeviceIdType.MESH


def next_lon(x):
    return pltpu.roll(x, LON - 1, 1)


def prev_lon(x):
    return pltpu.roll(x, 1, 1)


def next_row(x):
    return pltpu.roll(x, 2 * ROWS - 1, 0)


def prev_row(x):
    return pltpu.roll(x, 1, 0)


def advance(east, north, height):
    diff_east = 0.1 * (next_lon(east) - prev_lon(east))
    diff_north = 0.1 * (next_lon(north) - prev_lon(north))
    diff_height = 0.1 * (next_lon(height) - prev_lon(height))
    return (
        east - (east * diff_east + diff_height),
        north - east * diff_north,
        height - (east * diff_height + diff_east),
    )


def adjoint_step(state, adjoint, keep):
    east, north, height = state
    a, b, c = adjoint
    depth = 0.1 * jnp.exp(0.25 * height)
    visc = 0.04 + 0.02 * jnp.tanh(height)
    east, north = 0.1 * east, 0.1 * north
    c_next, c_prev = visc + east, visc - east
    r_next, r_prev = visc + north, visc - north
    middle = 1.0 - 4.0 * visc

    def spread(f, zonal=None, merid=None):
        if zonal is None:
            zonal = merid = 0.0
        return (
            middle * f
            + next_lon(c_next * f + zonal)
            + prev_lon(c_prev * f - zonal)
            + next_row(r_next * f + merid)
            + prev_row(r_prev * f - merid)
        )

    new_a = spread(a) + depth * (next_lon(c) - prev_lon(c))
    new_b = spread(b) + depth * (next_row(c) - prev_row(c))
    new_c = spread(c, 0.1 * a, 0.1 * b)
    return tuple(jnp.where(keep, f, 0.0) for f in (new_a, new_b, new_c))


def kernel(
    index_hbm, seed_ref, ckpt, innov, out,
    index_ref,
    p_row, p_col, p_last, p_mine, p_edge,
    q_col, q_row, q_last, q_mine, q_edge,
    own, edge, force, force_edge,
    p_sem, q_sem, gather_sem, far_sem, spread_sem, edge_sem, force_sem, local_sem,
):
    band = lax.axis_index("band")
    member = lax.axis_index("member")
    y, z = lax.rem(member, NY), member // NY
    is_low, is_high = band == LOW_FAR, band == HIGH_FAR
    is_far = jnp.logical_or(is_low, is_high)
    near_up = jnp.logical_and(band < NBAND - 1, jnp.logical_not(is_low))
    near_down = jnp.logical_and(band > 0, jnp.logical_not(is_high))
    at_end = jnp.logical_or(band == 0, band == NBAND - 1)
    up, down = {"band": band + 1}, {"band": band - 1}
    far = {"band": NBAND - 1 - band, "member": (NZ - 1 - z) * NY + y}

    y_peers = [lax.rem(y + step, NY) for step in range(1, NY)]
    z_peers = [lax.rem(z + step, NZ) for step in range(1, NZ)]

    def at_y(peer):
        return {"member": z * NY + peer}

    def at_z(peer):
        return {"member": peer * NY + y}

    def low_rows(k):
        return slice(0, EDGE[k])

    def high_rows(k):
        return slice(ROWS - EDGE[k], ROWS)

    def p_part(peer, rows=slice(None)):
        planes = pl.ds((HALF // 2) * (peer // 4), HALF // 2)
        return planes, rows, pl.ds(pl.multiple_of(128 * lax.rem(peer, 4), 128), 128)

    def q_part(peer, rows=slice(None)):
        return HALF + peer, rows

    def send(src, dst, sems, device):
        return pltpu.make_async_remote_copy(
            src_ref=src, dst_ref=dst, send_sem=sems.at[0], recv_sem=sems.at[1],
            device_id=device, device_id_type=MESH,
        )

    def drain(ref, sems):
        return send(ref, ref, sems, at_y(y_peers[0]))

    def copy(src, dst, slot):
        return pltpu.make_async_copy(src, dst, local_sem.at[slot])

    load_index = copy(index_hbm, index_ref, 11)
    load = copy(innov, force, 0)
    load_index.start()
    load.start()
    edge[...] = jnp.zeros_like(edge)
    force_edge[...] = jnp.zeros_like(force_edge)

    barrier = pltpu.get_barrier_semaphore()

    def greet(device):
        pl.semaphore_signal(barrier, inc=1, device_id=device, device_id_type=MESH)

    for peer in z_peers:
        greet(at_z(peer))
    for peer in y_peers:
        greet(at_y(peer))
    pl.when(near_up)(lambda: greet(up))
    pl.when(near_down)(lambda: greet(down))
    pl.when(is_far)(lambda: greet(far))
    pl.when(at_end)(lambda: pl.semaphore_wait(barrier, NY + NZ - 1))
    pl.when(jnp.logical_not(at_end))(lambda: pl.semaphore_wait(barrier, NY + NZ))

    for peer in z_peers:
        send(ckpt.at[q_part(peer)], q_col.at[z], q_sem.at[0], at_z(peer)).start()
    for peer in y_peers:
        send(ckpt.at[p_part(peer)], p_row.at[y], p_sem.at[0], at_y(peer)).start()
    p_keep = copy(ckpt.at[p_part(y)], p_row.at[y], 1)
    q_keep = copy(ckpt.at[q_part(z)], q_col.at[z], 2)
    p_keep.start()
    q_keep.start()

    def edge_up(src, dst, sems, k, device):
        rows = (k, slice(None), high_rows(k))
        return send(src(k, high_rows(k)), dst.at[rows], sems.at[k, 0], device)

    def edge_down(src, dst, sems, k, device):
        rows = (k, slice(None), low_rows(k))
        return send(src(k, low_rows(k)), dst.at[rows], sems.at[k, 1], device)

    def start_edges(src, dst, sems, k, with_far):
        pl.when(near_up)(lambda: edge_up(src, dst, sems, k, up).start())
        pl.when(near_down)(lambda: edge_down(src, dst, sems, k, down).start())
        if with_far:
            pl.when(is_low)(lambda: edge_up(src, dst, sems, k, far).start())
            pl.when(is_high)(lambda: edge_down(src, dst, sems, k, far).start())

    def finish_edges(src, dst, sems, k, with_far):
        def upper():
            edge_up(src, dst, sems, k, up).wait_send()
            edge_down(src, dst, sems, k, up).wait_recv()

        def lower():
            edge_down(src, dst, sems, k, down).wait_send()
            edge_up(src, dst, sems, k, down).wait_recv()

        pl.when(near_up)(upper)
        pl.when(near_down)(lower)
        if with_far:
            pl.when(is_low)(upper)
            pl.when(is_high)(lower)

    def innov_rows(k, rows):
        return innov.at[k, :, rows]

    def own_rows(k, rows):
        return own.at[k, :, rows]

    for k in (1, 0):
        start_edges(innov_rows, force_edge, force_sem, k, True)

    load_index.wait()
    seed = seed_ref[0]
    index = [index_ref[0], index_ref[1]]
    other = jnp.where(index[0] == LAST_SLOT, index[1], index[0])
    load.wait()
    for k in range(2):
        for plane in range(PLANES):
            force[k, plane] = pltpu.roll(force[k, plane], seed, 1)

    p_keep.wait()
    drain(p_row.at[pl.ds(0, NY - 1)], p_sem.at[0]).wait()
    p_col[z] = p_row[lax.rem(other, NY)]
    for peer in z_peers:
        send(p_col.at[z], p_col.at[z], p_sem.at[1], at_z(peer)).start()

    @pl.when(z == NZ - 1)
    def _():
        p_last[...] = p_row[NY - 1]
        for peer in z_peers:
            send(p_last, p_last, p_sem.at[2], at_z(peer)).start()

    q_keep.wait()
    drain(q_col.at[pl.ds(0, NZ - 1)], q_sem.at[0]).wait()
    q_row[y] = q_col[other // NY]
    for peer in y_peers:
        send(q_row.at[y], q_row.at[y], q_sem.at[1], at_y(peer)).start()

    @pl.when(y == NY - 1)
    def _():
        q_last[...] = q_col[NZ - 1]
        for peer in y_peers:
            send(q_last, q_last, q_sem.at[2], at_y(peer)).start()

    drain(p_col.at[pl.ds(0, NZ - 1)], p_sem.at[1]).wait()
    pl.when(z == NZ - 1)(lambda: drain(p_col.at[pl.ds(0, NZ - 1)], p_sem.at[2]).wait_send())
    pl.when(z < NZ - 1)(lambda: drain(p_last, p_sem.at[2]).wait_recv())
    from_other, from_last = p_col[other // NY], p_last[...]
    for k in (1, 0):
        p_mine[k] = jnp.where(index[k] == LAST_SLOT, from_last, from_other)
    keeps = []
    for k in (1, 0):
        for peer in y_peers:
            send(p_mine.at[k], own.at[(k,) + p_part(y)], gather_sem.at[k, 0], at_y(peer)).start()
        keeps.append(copy(p_mine.at[k], own.at[(k,) + p_part(y)], 3 + k))
        keeps[-1].start()

    def far_rows(mine, landing, sems, job):
        for k in (1, 0):
            def low():
                rows = (k,) + (slice(None),) * (len(mine.shape) - 3)
                getattr(send(mine.at[rows + (high_rows(k),)], landing.at[rows + (high_rows(k),)], sems.at[k], far), job)()

            def high():
                rows = (k,) + (slice(None),) * (len(mine.shape) - 3)
                getattr(send(mine.at[rows + (low_rows(k),)], landing.at[rows + (low_rows(k),)], sems.at[k], far), job)()

            if job == "wait_recv":
                low, high = high, low
            pl.when(is_low)(low)
            pl.when(is_high)(high)

    far_rows(p_mine, p_edge, far_sem.at[0], "start")

    drain(q_row.at[pl.ds(0, NY - 1)], q_sem.at[1]).wait()
    pl.when(y == NY - 1)(lambda: drain(q_row.at[pl.ds(0, NY - 1)], q_sem.at[2]).wait_send())
    pl.when(y < NY - 1)(lambda: drain(q_last, q_sem.at[2]).wait_recv())
    from_other, from_last = q_row[lax.rem(other, NY)], q_last[...]
    for k in (1, 0):
        q_mine[k] = jnp.where(index[k] == LAST_SLOT, from_last, from_other)
    for k in (1, 0):
        for peer in z_peers:
            send(q_mine.at[k], own.at[(k,) + q_part(z)], gather_sem.at[k, 1], at_z(peer)).start()
        keeps.append(copy(q_mine.at[k], own.at[(k,) + q_part(z)], 5 + k))
        keeps[-1].start()
    far_rows(q_mine, q_edge, far_sem.at[1], "start")

    far_rows(p_mine, p_edge, far_sem.at[0], "wait_recv")
    for k in (1, 0):
        def pass_p(rows):
            for peer in y_peers:
                send(p_edge.at[k, :, rows], edge.at[(k,) + p_part(y, rows)], spread_sem.at[k, 0], at_y(peer)).start()
            copy(p_edge.at[k, :, rows], edge.at[(k,) + p_part(y, rows)], 7 + k).start()

        pl.when(is_low)(lambda: pass_p(low_rows(k)))
        pl.when(is_high)(lambda: pass_p(high_rows(k)))
    far_rows(q_mine, q_edge, far_sem.at[1], "wait_recv")
    for k in (1, 0):
        def pass_q(rows):
            for peer in z_peers:
                send(q_edge.at[k, rows], edge.at[(k,) + q_part(NZ - 1 - z, rows)], spread_sem.at[k, 1], at_z(peer)).start()
            copy(q_edge.at[k, rows], edge.at[(k,) + q_part(NZ - 1 - z, rows)], 9 + k).start()

        pl.when(is_low)(lambda: pass_q(low_rows(k)))
        pl.when(is_high)(lambda: pass_q(high_rows(k)))

    for k in (1, 0):
        finish_edges(innov_rows, force_edge, force_sem, k, True)
        for plane in range(PLANES):
            force_edge[k, plane] = pltpu.roll(force_edge[k, plane], seed, 1)

    for job in keeps:
        job.wait()
    for k in (1, 0):
        drain(p_row.at[pl.ds(0, NY - 1)], gather_sem.at[k, 0]).wait()
        drain(q_col.at[pl.ds(0, NZ - 1)], gather_sem.at[k, 1]).wait()
        start_edges(own_rows, edge, edge_sem, k, False)

    row = lax.broadcasted_iota(jnp.int32, (2 * ROWS, LON), 0)
    outside = jnp.logical_or(
        jnp.logical_and(band == NBAND - 1, jnp.logical_and(row >= 8, row < 12)),
        jnp.logical_and(band == 0, row >= 12),
    )
    keep = jnp.logical_not(outside)

    adjoint = [None] * LEV
    for k in (1, 0):
        finish_edges(own_rows, edge, edge_sem, k, False)

        @pl.when(is_far)
        def _():
            rows = low_rows(k)
            drain(p_row.at[pl.ds(0, NY - 1), :, rows], spread_sem.at[k, 0]).wait()
            drain(q_col.at[pl.ds(0, NZ - 1), rows], spread_sem.at[k, 1]).wait()
            copy(p_edge.at[k, :, rows], p_edge.at[k, :, rows], 7 + k).wait()
            copy(q_edge.at[k, rows], q_edge.at[k, rows], 9 + k).wait()

        for lev in range(LEV):
            def both(inner, outer):
                return tuple(
                    jnp.concatenate([inner[k, comp * LEV + lev], outer[k, comp * LEV + lev]], axis=0)
                    for comp in range(3)
                )

            forcing = both(force, force_edge)
            if adjoint[lev] is None:
                field = forcing
            else:
                field = tuple(f + g for f, g in zip(adjoint[lev], forcing))
            first = both(own, edge)
            field = adjoint_step(advance(*first), field, keep)
            field = adjoint_step(first, field, keep)
            if k == 1:
                adjoint[lev] = field
            else:
                for comp in range(3):
                    out[comp * LEV + lev] = field[comp][:ROWS]

    far_rows(p_mine, p_edge, far_sem.at[0], "wait_send")
    far_rows(q_mine, q_edge, far_sem.at[1], "wait_send")


def on_device(checkpoints, ckpt_index, innovations, seeds):
    slot = checkpoints.reshape(PLANES, ROWS, LON)
    current = innovations.reshape(2, PLANES, ROWS, LON)
    hbm = pl.BlockSpec(memory_space=pltpu.HBM)
    slot, current, ckpt_index = (
        pltpu.with_memory_space_constraint(operand, pltpu.HBM) for operand in (slot, current, ckpt_index)
    )
    field = (2, PLANES, ROWS, LON)
    dma = pltpu.SemaphoreType.DMA

    def vmem(*shape):
        return pltpu.VMEM(shape, jnp.float32)

    result = pl.pallas_call(
        kernel,
        out_shape=jax.ShapeDtypeStruct((PLANES, ROWS, LON), jnp.float32),
        in_specs=[hbm, pl.BlockSpec(memory_space=pltpu.SMEM), hbm, hbm],
        out_specs=pl.BlockSpec(memory_space=pltpu.VMEM),
        scratch_shapes=[
            pltpu.SMEM((2,), jnp.int32),
            vmem(NY, HALF // 2, ROWS, 128),
            vmem(NZ, HALF // 2, ROWS, 128),
            vmem(HALF // 2, ROWS, 128),
            vmem(2, HALF // 2, ROWS, 128),
            vmem(2, HALF // 2, ROWS, 128),
            vmem(NZ, ROWS, LON),
            vmem(NY, ROWS, LON),
            vmem(ROWS, LON),
            vmem(2, ROWS, LON),
            vmem(2, ROWS, LON),
            vmem(*field),
            vmem(*field),
            vmem(*field),
            vmem(*field),
            dma((3, 2)),
            dma((3, 2)),
            dma((2, 2, 2)),
            dma((2, 2, 2)),
            dma((2, 2, 2)),
            dma((2, 2, 2)),
            dma((2, 2, 2)),
            dma((12,)),
        ],
        compiler_params=pltpu.CompilerParams(
            collective_id=0, has_side_effects=True, vmem_limit_bytes=32 * 2**20
        ),
        name="ensemble_adjoint",
    )(ckpt_index, seeds, slot, current)
    return result.reshape(1, 3, LEV, ROWS, LON)


def solution(mesh):
    return jax.shard_map(
        on_device,
        mesh=mesh,
        in_specs=(
            P("member", None, None, "band", None),
            P(),
            P(None, None, None, "band", None),
            P("member"),
        ),
        out_specs=P("member", None, None, "band", None),
        check_vma=False,
    )
```

time: 56.9 us -> 43.5 us (0.76)
  the two profiles are of different devices: /device:TPU:71 before, /device:TPU:7 now
where the time goes in v2:
time: 43.5 us; the launch traced here: 43.3 us
  Pallas kernels  42 us (97%)
  local copies, waits for them, and re-layouts  0.68 us (2%)
  between operations  0.66 us (2%)
    pallas_call x1, Pallas kernels, on_device(): pl.pallas_call(kernel, out_shape=jax.ShapeDtypeStruct((PLANES, ROWS, LON)...  42 us

profile of v2, /device:TPU:7, one launch (start us, length us, event | category | flops | bytes accessed | tf_op | source)
XLA Modules:
  0.0 43.3 jit_solution(6837441231912599764)
XLA Ops:
  0.7 42.0 %ensemble_adjoint.1 = f32[12,8,512]{2,1,0:T(8,128)S(1)} custom-call(s32[2]{0:T(128)} %index_hbm.1, s32[1]{0:T(128)S(6)} %copy.6.seed_ref, f32[12,8,512]{2,1,0:T(8,128)} %bitcast.5, f32[2,12,8,512]{3,2,1,0:T(8,128)} %bitcast.4), custom_call_target="tpu_custom_call" | custom-call | tf_op jit(solution)/shard_map/ensemble_adjoint/pallas_call | solution.py:363
  42.6 0.7 %copy.7 = f32[1,3,4,8,512]{4,3,2,1,0:T(8,128)} copy(f32[1,3,4,8,512]{4,3,2,1,0:T(8,128)S(1)} %bitcast.3) | data formatting | bytes 393216

commit v3 on v2

v3 whole, which is shorter than its diff:
```python
import jax
import jax.numpy as jnp
from jax import lax
from jax.experimental import pallas as pl
from jax.experimental.pallas import tpu as pltpu
from jax.sharding import PartitionSpec as P

NY = 8
NZ = 6
NBAND = 16
LOW_FAR, HIGH_FAR = NBAND // 2 - 1, NBAND // 2
LEV = 4
PLANES = 3 * LEV
HALF = PLANES // 2
ROWS = 8
LON = 512
LAST_SLOT = NY * NZ - 1
EDGE = {1: 4, 0: 2}
MESH = pl.DeviceIdType.MESH


def next_lon(x):
    return pltpu.roll(x, LON - 1, 1)


def prev_lon(x):
    return pltpu.roll(x, 1, 1)


def next_row(x):
    return pltpu.roll(x, 2 * ROWS - 1, 0)


def prev_row(x):
    return pltpu.roll(x, 1, 0)


def advance(east, north, height):
    diff_east = 0.1 * (next_lon(east) - prev_lon(east))
    diff_north = 0.1 * (next_lon(north) - prev_lon(north))
    diff_height = 0.1 * (next_lon(height) - prev_lon(height))
    return (
        east - (east * diff_east + diff_height),
        north - east * diff_north,
        height - (east * diff_height + diff_east),
    )


def adjoint_step(state, adjoint, keep):
    east, north, height = state
    a, b, c = adjoint
    depth = 0.1 * jnp.exp(0.25 * height)
    visc = 0.04 + 0.02 * jnp.tanh(height)
    east, north = 0.1 * east, 0.1 * north
    c_next, c_prev = visc + east, visc - east
    r_next, r_prev = visc + north, visc - north
    middle = 1.0 - 4.0 * visc

    def spread(f, zonal=None, merid=None):
        if zonal is None:
            zonal = merid = 0.0
        return (
            middle * f
            + next_lon(c_next * f + zonal)
            + prev_lon(c_prev * f - zonal)
            + next_row(r_next * f + merid)
            + prev_row(r_prev * f - merid)
        )

    new_a = spread(a) + depth * (next_lon(c) - prev_lon(c))
    new_b = spread(b) + depth * (next_row(c) - prev_row(c))
    new_c = spread(c, 0.1 * a, 0.1 * b)
    return tuple(jnp.where(keep, f, 0.0) for f in (new_a, new_b, new_c))


def kernel(
    index_hbm, seed_ref, ckpt, innov, out,
    index_ref, slot,
    p_row, p_col, p_last, p_mine, p_edge,
    q_col, q_row, q_last, q_mine, q_edge,
    h_slot, h_row, h_col, h_last, h_mine,
    own, edge, force, force_edge,
    p_sem, q_sem, h_sem, gather_sem, cross_sem, spread_sem, h_gather_sem, edge_sem, force_sem, local_sem,
):
    band = lax.axis_index("band")
    member = lax.axis_index("member")
    y, z = lax.rem(member, NY), member // NY
    odd = lax.rem(band, 2) == 1
    even = jnp.logical_not(odd)
    is_low, is_high = band == LOW_FAR, band == HIGH_FAR
    is_far = jnp.logical_or(is_low, is_high)
    near_up = jnp.logical_and(band < NBAND - 1, jnp.logical_not(is_low))
    near_down = jnp.logical_and(band > 0, jnp.logical_not(is_high))
    cross_up, cross_down = jnp.logical_and(odd, near_up), jnp.logical_and(even, near_down)
    at_end = jnp.logical_or(band == 0, band == NBAND - 1)
    up, down = {"band": band + 1}, {"band": band - 1}
    far = {"band": NBAND - 1 - band, "member": (NZ - 1 - z) * NY + y}

    y_peers = [lax.rem(y + step, NY) for step in range(1, NY)]
    z_peers = [lax.rem(z + step, NZ) for step in range(1, NZ)]

    def at_y(peer):
        return {"member": z * NY + peer}

    def at_z(peer):
        return {"member": peer * NY + y}

    def low_rows(k):
        return slice(0, EDGE[k])

    def high_rows(k):
        return slice(ROWS - EDGE[k], ROWS)

    def p_part(peer, rows=slice(None)):
        planes = pl.ds((HALF // 2) * (peer // 4), HALF // 2)
        return planes, rows, pl.ds(pl.multiple_of(128 * lax.rem(peer, 4), 128), 128)

    def q_part(peer, rows=slice(None)):
        return HALF + peer, rows

    def h_part(peer, rows):
        planes = pl.ds(HALF * (peer // 4), HALF)
        return planes, rows, pl.ds(pl.multiple_of(128 * lax.rem(peer, 4), 128), 128)

    def send(src, dst, sems, device):
        return pltpu.make_async_remote_copy(
            src_ref=src, dst_ref=dst, send_sem=sems.at[0], recv_sem=sems.at[1],
            device_id=device, device_id_type=MESH,
        )

    def drain(ref, sems):
        return send(ref, ref, sems, at_y(y_peers[0]))

    def copy(src, dst, number):
        return pltpu.make_async_copy(src, dst, local_sem.at[number])

    def both_sides(at_odd, at_even, job):
        pl.when(at_odd)(lambda: job(high_rows, low_rows, up))
        pl.when(at_even)(lambda: job(low_rows, high_rows, down))

    barrier = pltpu.get_barrier_semaphore()

    def greet(device):
        pl.semaphore_signal(barrier, inc=1, device_id=device, device_id_type=MESH)

    for peer in z_peers:
        greet(at_z(peer))
    for peer in y_peers:
        greet(at_y(peer))
    pl.when(near_up)(lambda: greet(up))
    pl.when(near_down)(lambda: greet(down))
    pl.when(is_far)(lambda: greet(far))

    load_slot = copy(ckpt, slot, 0)
    load_index = copy(index_hbm, index_ref, 1)
    load_force = copy(innov, force, 2)
    load_slot.start()
    load_index.start()
    load_force.start()
    load_slot.wait()
    p_row[y] = slot[p_part(y)]
    q_col[z] = slot[q_part(z)]

    pl.when(at_end)(lambda: pl.semaphore_wait(barrier, NY + NZ - 1))
    pl.when(jnp.logical_not(at_end))(lambda: pl.semaphore_wait(barrier, NY + NZ))

    for peer in z_peers:
        send(slot.at[q_part(peer)], q_col.at[z], q_sem.at[0], at_z(peer)).start()
    for peer in y_peers:
        send(slot.at[p_part(peer)], p_row.at[y], p_sem.at[0], at_y(peer)).start()

    def far_slot(sent, got, device):
        send(slot.at[:, sent(1)], h_slot.at[:, sent(1)], h_sem.at[0], far).start()

    both_sides(is_low, is_high, far_slot)

    def edge_up(src, dst, sems, k, device):
        rows = (k, slice(None), high_rows(k))
        return send(src.at[rows], dst.at[rows], sems.at[k, 0], device)

    def edge_down(src, dst, sems, k, device):
        rows = (k, slice(None), low_rows(k))
        return send(src.at[rows], dst.at[rows], sems.at[k, 1], device)

    def start_edges(src, dst, sems, k, upward, downward):
        pl.when(upward)(lambda: edge_up(src, dst, sems, k, up).start())
        pl.when(downward)(lambda: edge_down(src, dst, sems, k, down).start())

    def finish_edges(src, dst, sems, k, upward, downward):
        def upper():
            edge_up(src, dst, sems, k, up).wait_send()
            edge_down(src, dst, sems, k, up).wait_recv()

        def lower():
            edge_down(src, dst, sems, k, down).wait_send()
            edge_up(src, dst, sems, k, down).wait_recv()

        pl.when(upward)(upper)
        pl.when(downward)(lower)

    for k in (1, 0):
        start_edges(innov, force_edge, force_sem, k, near_up, near_down)
        pl.when(is_low)(lambda: edge_up(innov, force_edge, force_sem, k, far).start())
        pl.when(is_high)(lambda: edge_down(innov, force_edge, force_sem, k, far).start())

    load_index.wait()
    seed = seed_ref[0]
    index = [index_ref[0], index_ref[1]]
    other = jnp.where(index[0] == LAST_SLOT, index[1], index[0])
    other_y, other_z = lax.rem(other, NY), other // NY
    load_force.wait()
    for k in range(2):
        for plane in range(PLANES):
            force[k, plane] = pltpu.roll(force[k, plane], seed, 1)

    drain(p_row.at[pl.ds(0, NY - 1)], p_sem.at[0]).wait()
    p_col[z] = p_row[other_y]
    for peer in z_peers:
        send(p_col.at[z], p_col.at[z], p_sem.at[1], at_z(peer)).start()

    @pl.when(z == NZ - 1)
    def _():
        p_last[...] = p_row[NY - 1]
        for peer in z_peers:
            send(p_last, p_last, p_sem.at[2], at_z(peer)).start()

    drain(q_col.at[pl.ds(0, NZ - 1)], q_sem.at[0]).wait()
    q_row[y] = q_col[other_z]
    for peer in y_peers:
        send(q_row.at[y], q_row.at[y], q_sem.at[1], at_y(peer)).start()

    @pl.when(y == NY - 1)
    def _():
        q_last[...] = q_col[NZ - 1]
        for peer in y_peers:
            send(q_last, q_last, q_sem.at[2], at_y(peer)).start()

    def far_row(sent, got, device):
        send(slot.at[:, sent(1)], h_slot.at[:, sent(1)], h_sem.at[0], far).wait_send()
        send(h_slot.at[:, got(1)], h_slot.at[:, got(1)], h_sem.at[0], far).wait_recv()
        for peer in y_peers:
            send(h_slot.at[h_part(peer, got(1))], h_row.at[y, :, got(1)], h_sem.at[1], at_y(peer)).start()
        h_row[y, :, got(1)] = h_slot[h_part(y, got(1))]

    both_sides(is_low, is_high, far_row)

    drain(p_col.at[pl.ds(0, NZ - 1)], p_sem.at[1]).wait()
    pl.when(z == NZ - 1)(lambda: drain(p_col.at[pl.ds(0, NZ - 1)], p_sem.at[2]).wait_send())
    pl.when(z < NZ - 1)(lambda: drain(p_last, p_sem.at[2]).wait_recv())
    from_other, from_last = p_col[other_z], p_last[...]
    for k in (1, 0):
        p_mine[k] = jnp.where(index[k] == LAST_SLOT, from_last, from_other)

    def cross_p(sent, got, device):
        send(p_mine.at[0, :, sent(0)], p_edge.at[:, sent(0)], cross_sem.at[0], device).start()

    both_sides(cross_up, cross_down, cross_p)
    for k in (1, 0):
        for peer in y_peers:
            send(p_mine.at[k], own.at[(k,) + p_part(y)], gather_sem.at[k, 0], at_y(peer)).start()
        own[(k,) + p_part(y)] = p_mine[k]

    def far_col(sent, got, device):
        drain(h_row.at[pl.ds(0, NY - 1), :, got(1)], h_sem.at[1]).wait()
        h_col[z, :, got(1)] = h_row[other_y, :, got(1)]
        for peer in z_peers:
            send(h_col.at[z, :, got(1)], h_col.at[z, :, got(1)], h_sem.at[2], at_z(peer)).start()

        @pl.when(z == 0)
        def _():
            h_last[:, got(1)] = h_row[NY - 1, :, got(1)]
            for peer in z_peers:
                send(h_last.at[:, got(1)], h_last.at[:, got(1)], h_sem.at[3], at_z(peer)).start()

    both_sides(is_low, is_high, far_col)

    drain(q_row.at[pl.ds(0, NY - 1)], q_sem.at[1]).wait()
    pl.when(y == NY - 1)(lambda: drain(q_row.at[pl.ds(0, NY - 1)], q_sem.at[2]).wait_send())
    pl.when(y < NY - 1)(lambda: drain(q_last, q_sem.at[2]).wait_recv())
    from_other, from_last = q_row[other_y], q_last[...]
    for k in (1, 0):
        q_mine[k] = jnp.where(index[k] == LAST_SLOT, from_last, from_other)

    def cross_q(sent, got, device):
        send(q_mine.at[0, sent(0)], q_edge.at[sent(0)], cross_sem.at[1], device).start()

    both_sides(cross_up, cross_down, cross_q)
    for k in (1, 0):
        for peer in z_peers:
            send(q_mine.at[k], own.at[(k,) + q_part(z)], gather_sem.at[k, 1], at_z(peer)).start()
        own[(k,) + q_part(z)] = q_mine[k]

    def spread_p(sent, got, device):
        drain(p_edge.at[:, got(0)], cross_sem.at[0]).wait()
        for peer in y_peers:
            send(p_edge.at[:, got(0)], edge.at[(0,) + p_part(y, got(0))], spread_sem.at[0], at_y(peer)).start()
        edge[(0,) + p_part(y, got(0))] = p_edge[:, got(0)]

    def spread_q(sent, got, device):
        drain(q_edge.at[got(0)], cross_sem.at[1]).wait()
        for peer in z_peers:
            send(q_edge.at[got(0)], edge.at[(0,) + q_part(z, got(0))], spread_sem.at[1], at_z(peer)).start()
        edge[(0,) + q_part(z, got(0))] = q_edge[got(0)]

    both_sides(cross_up, cross_down, spread_p)
    both_sides(cross_up, cross_down, spread_q)

    def far_gather(sent, got, device):
        drain(h_col.at[pl.ds(0, NZ - 1), :, got(1)], h_sem.at[2]).wait()
        pl.when(z == 0)(lambda: drain(h_col.at[pl.ds(0, NZ - 1), :, got(1)], h_sem.at[3]).wait_send())
        pl.when(z > 0)(lambda: drain(h_last.at[:, got(1)], h_sem.at[3]).wait_recv())
        from_other, from_last = h_col[NZ - 1 - other_z, :, got(1)], h_last[:, got(1)]
        for k in (1, 0):
            h_mine[k, :, got(1)] = jnp.where(index[k] == LAST_SLOT, from_last, from_other)
            for peer in y_peers:
                send(
                    h_mine.at[k, :, got(k)], edge.at[(k,) + h_part(y, got(k))], h_gather_sem.at[k], at_y(peer)
                ).start()
            edge[(k,) + h_part(y, got(k))] = h_mine[k, :, got(k)]

    both_sides(is_low, is_high, far_gather)

    for k in (1, 0):
        finish_edges(innov, force_edge, force_sem, k, band < NBAND - 1, band > 0)
        for plane in range(PLANES):
            force_edge[k, plane] = pltpu.roll(force_edge[k, plane], seed, 1)

    needs_up, needs_down = {1: near_up, 0: even}, {1: near_down, 0: odd}
    for k in (1, 0):
        drain(p_row.at[pl.ds(0, NY - 1)], gather_sem.at[k, 0]).wait()
        drain(q_col.at[pl.ds(0, NZ - 1)], gather_sem.at[k, 1]).wait()
        start_edges(own, edge, edge_sem, k, needs_up[k], needs_down[k])

    row = lax.broadcasted_iota(jnp.int32, (ROWS, LON), 0)
    inside = jnp.logical_not(
        jnp.logical_or(
            jnp.logical_and(band == NBAND - 1, row < ROWS // 2),
            jnp.logical_and(band == 0, row >= ROWS // 2),
        )
    )
    keep = jnp.logical_or(
        lax.broadcasted_iota(jnp.int32, (2 * ROWS, LON), 0) < ROWS,
        jnp.concatenate([inside, inside], axis=0),
    )

    adjoint = [None] * LEV
    for k in (1, 0):
        finish_edges(own, edge, edge_sem, k, needs_up[k], needs_down[k])
        if k == 0:
            def spread_done(sent, got, device):
                drain(p_row.at[pl.ds(0, NY - 1), :, got(0)], spread_sem.at[0]).wait()
                drain(q_col.at[pl.ds(0, NZ - 1), got(0)], spread_sem.at[1]).wait()

            both_sides(cross_up, cross_down, spread_done)

        def far_done(sent, got, device):
            drain(h_row.at[pl.ds(0, NY - 1), :, got(k)], h_gather_sem.at[k]).wait()

        both_sides(is_low, is_high, far_done)

        for lev in range(LEV):
            def both(inner, outer):
                return tuple(
                    jnp.concatenate(
                        [inner[k, comp * LEV + lev], jnp.where(inside, outer[k, comp * LEV + lev], 0.0)], axis=0
                    )
                    for comp in range(3)
                )

            forcing = both(force, force_edge)
            if adjoint[lev] is None:
                field = forcing
            else:
                field = tuple(f + g for f, g in zip(adjoint[lev], forcing))
            first = both(own, edge)
            field = adjoint_step(advance(*first), field, keep)
            field = adjoint_step(first, field, keep)
            if k == 1:
                adjoint[lev] = field
            else:
                for comp in range(3):
                    out[comp * LEV + lev] = field[comp][:ROWS]


def on_device(checkpoints, ckpt_index, innovations, seeds):
    slot = checkpoints.reshape(PLANES, ROWS, LON)
    current = innovations.reshape(2, PLANES, ROWS, LON)
    hbm = pl.BlockSpec(memory_space=pltpu.HBM)
    slot, current, ckpt_index = (
        pltpu.with_memory_space_constraint(operand, pltpu.HBM) for operand in (slot, current, ckpt_index)
    )
    field = (2, PLANES, ROWS, LON)
    dma = pltpu.SemaphoreType.DMA

    def vmem(*shape):
        return pltpu.VMEM(shape, jnp.float32)

    result = pl.pallas_call(
        kernel,
        out_shape=jax.ShapeDtypeStruct((PLANES, ROWS, LON), jnp.float32),
        in_specs=[hbm, pl.BlockSpec(memory_space=pltpu.SMEM), hbm, hbm],
        out_specs=pl.BlockSpec(memory_space=pltpu.VMEM),
        scratch_shapes=[
            pltpu.SMEM((2,), jnp.int32),
            vmem(PLANES, ROWS, LON),
            vmem(NY, HALF // 2, ROWS, 128),
            vmem(NZ, HALF // 2, ROWS, 128),
            vmem(HALF // 2, ROWS, 128),
            vmem(2, HALF // 2, ROWS, 128),
            vmem(HALF // 2, ROWS, 128),
            vmem(NZ, ROWS, LON),
            vmem(NY, ROWS, LON),
            vmem(ROWS, LON),
            vmem(2, ROWS, LON),
            vmem(ROWS, LON),
            vmem(PLANES, ROWS, LON),
            vmem(NY, HALF, ROWS, 128),
            vmem(NZ, HALF, ROWS, 128),
            vmem(HALF, ROWS, 128),
            vmem(2, HALF, ROWS, 128),
            vmem(*field),
            vmem(*field),
            vmem(*field),
            vmem(*field),
            dma((3, 2)),
            dma((3, 2)),
            dma((4, 2)),
            dma((2, 2, 2)),
            dma((2, 2)),
            dma((2, 2)),
            dma((2, 2)),
            dma((2, 2, 2)),
            dma((2, 2, 2)),
            dma((3,)),
        ],
        compiler_params=pltpu.CompilerParams(
            collective_id=0, has_side_effects=True, vmem_limit_bytes=32 * 2**20
        ),
        name="ensemble_adjoint",
    )(ckpt_index, seeds, slot, current)
    return result.reshape(1, 3, LEV, ROWS, LON)


def solution(mesh):
    return jax.shard_map(
        on_device,
        mesh=mesh,
        in_specs=(
            P("member", None, None, "band", None),
            P(),
            P(None, None, None, "band", None),
            P("member"),
        ),
        out_specs=P("member", None, None, "band", None),
        check_vma=False,
    )
```

time: 43.5 us -> 43.2 us (level)
  no operation moved by 1% of the time
where the time goes in v3:
time: 43.2 us; the launch traced here: 43 us
  Pallas kernels  41.7 us (97%)
  local copies, waits for them, and re-layouts  0.68 us (2%)
  between operations  0.66 us (2%)
    pallas_call x1, Pallas kernels, on_device(): pl.pallas_call(kernel, out_shape=jax.ShapeDtypeStruct((PLANES, ROWS, LON)...  41.7 us

profile of v3, /device:TPU:7, one launch (start us, length us, event | category | flops | bytes accessed | tf_op | source)
XLA Modules:
  0.0 43.0 jit_solution(4372970910826361359)
XLA Ops:
  0.7 41.7 %ensemble_adjoint.1 = f32[12,8,512]{2,1,0:T(8,128)S(1)} custom-call(s32[2]{0:T(128)} %index_hbm.1, s32[1]{0:T(128)S(6)} %copy.6.seed_ref, f32[12,8,512]{2,1,0:T(8,128)} %bitcast.5, f32[2,12,8,512]{3,2,1,0:T(8,128)} %bitcast.4), custom_call_target="tpu_custom_call" | custom-call | tf_op jit(solution)/shard_map/ensemble_adjoint/pallas_call | solution.py:398
  42.4 0.7 %copy.7 = f32[1,3,4,8,512]{4,3,2,1,0:T(8,128)} copy(f32[1,3,4,8,512]{4,3,2,1,0:T(8,128)S(1)} %bitcast.3) | data formatting | bytes 393216

commit v4 on v3

v4 whole, which is shorter than its diff:
```python
import functools

import jax
import jax.numpy as jnp
from jax import lax
from jax.experimental import pallas as pl
from jax.experimental.pallas import tpu as pltpu
from jax.sharding import PartitionSpec as P

NY = 8
NZ = 6
NBAND = 16
CHIPS = NBAND // 2
LEV = 4
PLANES = 3 * LEV
HALF = PLANES // 2
ROWS = 8
LON = 512
LAST_SLOT = NY * NZ - 1
EDGE = {1: 4, 0: 2}
MESH = pl.DeviceIdType.MESH


def next_lon(x):
    return pltpu.roll(x, LON - 1, 1)


def prev_lon(x):
    return pltpu.roll(x, 1, 1)


def next_row(x):
    return pltpu.roll(x, 2 * ROWS - 1, 0)


def prev_row(x):
    return pltpu.roll(x, 1, 0)


def advance(east, north, height):
    diff_east = 0.1 * (next_lon(east) - prev_lon(east))
    diff_north = 0.1 * (next_lon(north) - prev_lon(north))
    diff_height = 0.1 * (next_lon(height) - prev_lon(height))
    return (
        east - (east * diff_east + diff_height),
        north - east * diff_north,
        height - (east * diff_height + diff_east),
    )


def adjoint_step(state, adjoint, keep):
    east, north, height = state
    a, b, c = adjoint
    depth = 0.1 * jnp.exp(0.25 * height)
    visc = 0.04 + 0.02 * jnp.tanh(height)
    east, north = 0.1 * east, 0.1 * north
    c_next, c_prev = visc + east, visc - east
    r_next, r_prev = visc + north, visc - north
    middle = 1.0 - 4.0 * visc

    def spread(f, zonal=None, merid=None):
        if zonal is None:
            zonal = merid = 0.0
        return (
            middle * f
            + next_lon(c_next * f + zonal)
            + prev_lon(c_prev * f - zonal)
            + next_row(r_next * f + merid)
            + prev_row(r_prev * f - merid)
        )

    new_a = spread(a) + depth * (next_lon(c) - prev_lon(c))
    new_b = spread(b) + depth * (next_row(c) - prev_row(c))
    new_c = spread(c, 0.1 * a, 0.1 * b)
    return tuple(jnp.where(keep, f, 0.0) for f in (new_a, new_b, new_c))


def kernel(
    index_hbm, seed_ref, ckpt, innov, out,
    index_ref, slot,
    p_row, p_col, p_last, p_mine, p_edge,
    q_col, q_row, q_last, q_mine, q_edge,
    own, edge, force, force_edge,
    p_sem, q_sem, gather_sem, cross_sem, spread_sem, edge_sem, force_sem, local_sem,
):
    band = lax.axis_index("band")
    member = lax.axis_index("member")
    y, z = lax.rem(member, NY), member // NY
    chip = band // 2
    odd = lax.rem(band, 2) == 1
    even = jnp.logical_not(odd)
    has_up, has_down = band < NBAND - 1, band > 0
    chip_up, chip_down = chip < CHIPS - 1, chip > 0
    far_up, far_down = chip == CHIPS // 2 - 1, chip == CHIPS // 2
    z_above = jnp.where(far_up, NZ - 1 - z, z)
    z_below = jnp.where(far_down, NZ - 1 - z, z)
    member_up = z_above * NY + y
    member_down = z_below * NY + y

    y_peers = [lax.rem(y + step, NY) for step in range(1, NY)]
    z_peers = [lax.rem(z + step, NZ) for step in range(1, NZ)]
    low_band, high_band = 2 * chip, 2 * chip + 1

    def at_y(peer, of_band):
        return {"band": of_band, "member": z * NY + peer}

    def at_z(peer, of_band):
        return {"band": of_band, "member": peer * NY + y}

    sibling = {"band": low_band + high_band - band}
    up = {"band": band + 1, "member": jnp.where(odd, member_up, member)}
    down = {"band": band - 1, "member": jnp.where(odd, member, member_down)}
    handler_up = {"band": band + 2, "member": member_up}
    handler_down = {"band": band - 2, "member": member_down}

    def low_rows(k):
        return slice(0, EDGE[k])

    def high_rows(k):
        return slice(ROWS - EDGE[k], ROWS)

    def p_part(peer, rows=slice(None)):
        planes = pl.ds((HALF // 2) * (peer // 4), HALF // 2)
        return planes, rows, pl.ds(pl.multiple_of(128 * lax.rem(peer, 4), 128), 128)

    def q_part(peer, rows=slice(None)):
        return HALF + peer, rows

    def send(src, dst, sems, device):
        return pltpu.make_async_remote_copy(
            src_ref=src, dst_ref=dst, send_sem=sems.at[0], recv_sem=sems.at[1],
            device_id=device, device_id_type=MESH,
        )

    def drain(ref, sems):
        return send(ref, ref, sems, sibling)

    def p_pieces(count, rows=slice(None)):
        return p_row.at[pl.ds(0, count), :, rows]

    def q_planes(count, rows=slice(None)):
        return q_col.at[pl.ds(0, count), rows]

    def copy(src, dst, number):
        return pltpu.make_async_copy(src, dst, local_sem.at[number])

    barrier = pltpu.get_barrier_semaphore()

    def greet(device):
        pl.semaphore_signal(barrier, inc=1, device_id=device, device_id_type=MESH)

    for peer in z_peers:
        greet(at_z(peer, high_band))
    for peer in y_peers:
        greet(at_y(peer, high_band))
    greet(sibling)

    @pl.when(odd)
    def _():
        for peer in z_peers:
            greet(at_z(peer, low_band))
        for peer in y_peers:
            greet(at_y(peer, low_band))
        pl.when(chip_up)(lambda: greet(up))
        pl.when(chip_up)(lambda: greet(handler_up))
        pl.when(chip_down)(lambda: greet(handler_down))

    pl.when(jnp.logical_and(even, has_down))(lambda: greet(down))

    load_slot = copy(ckpt, slot, 0)
    load_index = copy(index_hbm, index_ref, 1)
    load_force = copy(innov, force, 2)
    load_slot.start()
    load_index.start()
    load_force.start()
    load_slot.wait()
    peers = NY + NZ - 2
    inner = jnp.logical_and(chip_up, chip_down)
    first, last = chip == 0, chip == CHIPS - 1
    for condition, count in (
        (jnp.logical_and(even, first), peers + 1),
        (jnp.logical_and(even, chip_down), peers + 2),
        (jnp.logical_and(odd, first), 2 * peers + 3),
        (jnp.logical_and(odd, last), 2 * peers + 2),
        (jnp.logical_and(odd, inner), 2 * peers + 4),
    ):
        pl.when(condition)(functools.partial(pl.semaphore_wait, barrier, count))

    def spots(core):
        return core * NZ + z, core * NY + y

    def first_phase(core):
        q_spot, p_spot = spots(core)
        for peer in z_peers:
            send(slot.at[q_part(peer)], q_col.at[q_spot], q_sem.at[0], at_z(peer, high_band)).start()
        for peer in y_peers:
            send(slot.at[p_part(peer)], p_row.at[p_spot], p_sem.at[0], at_y(peer, high_band)).start()
        if core == 0:
            send(slot.at[q_part(z)], q_col.at[q_spot], q_sem.at[0], sibling).start()
            send(slot.at[p_part(y)], p_row.at[p_spot], p_sem.at[0], sibling).start()
        else:
            p_row[p_spot] = slot[p_part(y)]
            q_col[q_spot] = slot[q_part(z)]

    pl.when(even)(lambda: first_phase(0))
    pl.when(odd)(lambda: first_phase(1))

    def edge_up(src, dst, sems, k, device):
        rows = (k, slice(None), high_rows(k))
        return send(src.at[rows], dst.at[rows], sems.at[k, 0], device)

    def edge_down(src, dst, sems, k, device):
        rows = (k, slice(None), low_rows(k))
        return send(src.at[rows], dst.at[rows], sems.at[k, 1], device)

    def start_edges(src, dst, sems, k, upward, downward):
        pl.when(upward)(lambda: edge_up(src, dst, sems, k, up).start())
        pl.when(downward)(lambda: edge_down(src, dst, sems, k, down).start())

    def finish_edges(src, dst, sems, k, upward, downward):
        def upper():
            edge_up(src, dst, sems, k, up).wait_send()
            edge_down(src, dst, sems, k, up).wait_recv()

        def lower():
            edge_down(src, dst, sems, k, down).wait_send()
            edge_up(src, dst, sems, k, down).wait_recv()

        pl.when(upward)(upper)
        pl.when(downward)(lower)

    for k in (1, 0):
        start_edges(innov, force_edge, force_sem, k, has_up, has_down)

    load_index.wait()
    seed = seed_ref[0]
    index = [index_ref[0], index_ref[1]]
    other = jnp.where(index[0] == LAST_SLOT, index[1], index[0])
    other_y, other_z = lax.rem(other, NY), other // NY
    load_force.wait()
    for k in range(2):
        for plane in range(PLANES):
            force[k, plane] = pltpu.roll(force[k, plane], seed, 1)

    @pl.when(odd)
    def _():
        drain(p_pieces(2 * NY - 1), p_sem.at[0]).wait_recv()
        for core in range(2):
            p_col[z, core] = p_row[core * NY + other_y]
        for peer in z_peers:
            send(p_col.at[z], p_col.at[z], p_sem.at[1], at_z(peer, high_band)).start()

        @pl.when(z == NZ - 1)
        def _():
            for core in range(2):
                p_last[core] = p_row[core * NY + NY - 1]
            for peer in z_peers:
                send(p_last, p_last, p_sem.at[2], at_z(peer, high_band)).start()

        drain(q_planes(2 * NZ - 1), q_sem.at[0]).wait_recv()
        for core in range(2):
            q_row[y, core] = q_col[core * NZ + other_z]
        for peer in y_peers:
            send(q_row.at[y], q_row.at[y], q_sem.at[1], at_y(peer, high_band)).start()

        @pl.when(y == NY - 1)
        def _():
            for core in range(2):
                q_last[core] = q_col[core * NZ + NZ - 1]
            for peer in y_peers:
                send(q_last, q_last, q_sem.at[2], at_y(peer, high_band)).start()

        def cross_up(mine, landing, kind, k, rows):
            return send(
                mine.at[(k, 1) + rows(high_rows(k))], landing.at[(1, k) + rows(high_rows(k))],
                cross_sem.at[0, kind, k], handler_up,
            )

        def cross_down(mine, landing, kind, k, rows):
            return send(
                mine.at[(k, 0) + rows(low_rows(k))], landing.at[(0, k) + rows(low_rows(k))],
                cross_sem.at[1, kind, k], handler_down,
            )

        def p_rows(rows):
            return slice(None), rows

        def q_rows(rows):
            return (rows,)

        def start_cross(*job):
            pl.when(chip_up)(lambda: cross_up(*job).start())
            pl.when(chip_down)(lambda: cross_down(*job).start())

        drain(p_col.at[pl.ds(0, NZ - 1)], p_sem.at[1]).wait()
        pl.when(z == NZ - 1)(lambda: drain(p_col.at[pl.ds(0, NZ - 1)], p_sem.at[2]).wait_send())
        pl.when(z < NZ - 1)(lambda: drain(p_last, p_sem.at[2]).wait_recv())
        from_other, from_last = p_col[other_z], p_last[...]
        for k in (1, 0):
            p_mine[k] = jnp.where(index[k] == LAST_SLOT, from_last, from_other)
            start_cross(p_mine, p_edge, 0, k, p_rows)
        for k in (1, 0):
            place = (k,) + p_part(y)
            send(p_mine.at[k, 0], own.at[place], gather_sem.at[k, 0], sibling).start()
            for peer in y_peers:
                send(p_mine.at[k, 0], own.at[place], gather_sem.at[k, 0], at_y(peer, low_band)).start()
                send(p_mine.at[k, 1], own.at[place], gather_sem.at[k, 0], at_y(peer, high_band)).start()
            own[place] = p_mine[k, 1]

        drain(q_row.at[pl.ds(0, NY - 1)], q_sem.at[1]).wait()
        pl.when(y == NY - 1)(lambda: drain(q_row.at[pl.ds(0, NY - 1)], q_sem.at[2]).wait_send())
        pl.when(y < NY - 1)(lambda: drain(q_last, q_sem.at[2]).wait_recv())
        from_other, from_last = q_row[other_y], q_last[...]
        for k in (1, 0):
            q_mine[k] = jnp.where(index[k] == LAST_SLOT, from_last, from_other)
            start_cross(q_mine, q_edge, 1, k, q_rows)
        for k in (1, 0):
            place = (k,) + q_part(z)
            send(q_mine.at[k, 0], own.at[place], gather_sem.at[k, 1], sibling).start()
            for peer in z_peers:
                send(q_mine.at[k, 0], own.at[place], gather_sem.at[k, 1], at_z(peer, low_band)).start()
                send(q_mine.at[k, 1], own.at[place], gather_sem.at[k, 1], at_z(peer, high_band)).start()
            own[place] = q_mine[k, 1]

        def spread_p(k):
            @pl.when(chip_down)
            def _():
                cross_up(p_mine, p_edge, 0, k, p_rows).wait_recv()
                piece, place = p_edge.at[1, k, :, high_rows(k)], (k,) + p_part(y, high_rows(k))
                send(piece, edge.at[place], spread_sem.at[0, k, 0], sibling).start()
                for peer in y_peers:
                    send(piece, edge.at[place], spread_sem.at[0, k, 0], at_y(peer, low_band)).start()

            @pl.when(chip_up)
            def _():
                cross_down(p_mine, p_edge, 0, k, p_rows).wait_recv()
                piece, place = p_edge.at[0, k, :, low_rows(k)], (k,) + p_part(y, low_rows(k))
                for peer in y_peers:
                    send(piece, edge.at[place], spread_sem.at[1, k, 0], at_y(peer, high_band)).start()
                edge[place] = p_edge[0, k, :, low_rows(k)]

        def spread_q(k):
            @pl.when(chip_down)
            def _():
                cross_up(q_mine, q_edge, 1, k, q_rows).wait_recv()
                piece, place = q_edge.at[1, k, high_rows(k)], (k,) + q_part(z_below, high_rows(k))
                send(piece, edge.at[place], spread_sem.at[0, k, 1], sibling).start()
                for peer in z_peers:
                    send(piece, edge.at[place], spread_sem.at[0, k, 1], at_z(peer, low_band)).start()

            @pl.when(chip_up)
            def _():
                cross_down(q_mine, q_edge, 1, k, q_rows).wait_recv()
                piece, place = q_edge.at[0, k, low_rows(k)], (k,) + q_part(z_above, low_rows(k))
                for peer in z_peers:
                    send(piece, edge.at[place], spread_sem.at[1, k, 1], at_z(peer, high_band)).start()
                edge[place] = q_edge[0, k, low_rows(k)]

        for k in (1, 0):
            spread_p(k)
        for k in (1, 0):
            spread_q(k)

    for k in (1, 0):
        finish_edges(innov, force_edge, force_sem, k, has_up, has_down)
        for plane in range(PLANES):
            force_edge[k, plane] = pltpu.roll(force_edge[k, plane], seed, 1)

    for k in (1, 0):
        @pl.when(odd)
        def _():
            drain(p_pieces(NY - 1), gather_sem.at[k, 0]).wait_recv()
            drain(q_planes(NZ - 1), gather_sem.at[k, 1]).wait_recv()

        @pl.when(even)
        def _():
            drain(p_pieces(NY), gather_sem.at[k, 0]).wait_recv()
            drain(q_planes(NZ), gather_sem.at[k, 1]).wait_recv()

        start_edges(own, edge, edge_sem, k, even, odd)

    row = lax.broadcasted_iota(jnp.int32, (ROWS, LON), 0)
    inside = jnp.logical_not(
        jnp.logical_or(
            jnp.logical_and(band == NBAND - 1, row < ROWS // 2),
            jnp.logical_and(band == 0, row >= ROWS // 2),
        )
    )
    keep = jnp.logical_or(
        lax.broadcasted_iota(jnp.int32, (2 * ROWS, LON), 0) < ROWS,
        jnp.concatenate([inside, inside], axis=0),
    )

    adjoint = [None] * LEV
    for k in (1, 0):
        @pl.when(jnp.logical_and(even, chip_down))
        def _():
            drain(p_pieces(NY, high_rows(k)), spread_sem.at[0, k, 0]).wait_recv()
            drain(q_planes(NZ, high_rows(k)), spread_sem.at[0, k, 1]).wait_recv()

        @pl.when(jnp.logical_and(odd, chip_up))
        def _():
            drain(p_pieces(NY - 1, low_rows(k)), spread_sem.at[1, k, 0]).wait_recv()
            drain(q_planes(NZ - 1, low_rows(k)), spread_sem.at[1, k, 1]).wait_recv()

        finish_edges(own, edge, edge_sem, k, even, odd)
        for lev in range(LEV):
            def both(inner_ref, outer_ref):
                return tuple(
                    jnp.concatenate(
                        [
                            inner_ref[k, comp * LEV + lev],
                            jnp.where(inside, outer_ref[k, comp * LEV + lev], 0.0),
                        ],
                        axis=0,
                    )
                    for comp in range(3)
                )

            forcing = both(force, force_edge)
            if adjoint[lev] is None:
                field = forcing
            else:
                field = tuple(f + g for f, g in zip(adjoint[lev], forcing))
            start = both(own, edge)
            field = adjoint_step(advance(*start), field, keep)
            field = adjoint_step(start, field, keep)
            if k == 1:
                adjoint[lev] = field
            else:
                for comp in range(3):
                    out[comp * LEV + lev] = field[comp][:ROWS]

    @pl.when(even)
    def _():
        drain(p_pieces(NY), p_sem.at[0]).wait_send()
        drain(q_planes(NZ), q_sem.at[0]).wait_send()

    @pl.when(odd)
    def _():
        drain(p_pieces(NY - 1), p_sem.at[0]).wait_send()
        drain(q_planes(NZ - 1), q_sem.at[0]).wait_send()
        for k in (1, 0):
            drain(p_pieces(2 * NY - 1), gather_sem.at[k, 0]).wait_send()
            drain(q_planes(2 * NZ - 1), gather_sem.at[k, 1]).wait_send()

            @pl.when(chip_up)
            def _():
                drain(p_edge.at[0, k, :, high_rows(k)], cross_sem.at[0, 0, k]).wait_send()
                drain(q_edge.at[0, k, high_rows(k)], cross_sem.at[0, 1, k]).wait_send()
                drain(p_pieces(NY - 1, low_rows(k)), spread_sem.at[1, k, 0]).wait_send()
                drain(q_planes(NZ - 1, low_rows(k)), spread_sem.at[1, k, 1]).wait_send()

            @pl.when(chip_down)
            def _():
                drain(p_edge.at[0, k, :, low_rows(k)], cross_sem.at[1, 0, k]).wait_send()
                drain(q_edge.at[0, k, low_rows(k)], cross_sem.at[1, 1, k]).wait_send()
                drain(p_pieces(NY, high_rows(k)), spread_sem.at[0, k, 0]).wait_send()
                drain(q_planes(NZ, high_rows(k)), spread_sem.at[0, k, 1]).wait_send()


def on_device(checkpoints, ckpt_index, innovations, seeds):
    slot = checkpoints.reshape(PLANES, ROWS, LON)
    current = innovations.reshape(2, PLANES, ROWS, LON)
    hbm = pl.BlockSpec(memory_space=pltpu.HBM)
    slot, current, ckpt_index = (
        pltpu.with_memory_space_constraint(operand, pltpu.HBM) for operand in (slot, current, ckpt_index)
    )
    field = (2, PLANES, ROWS, LON)
    dma = pltpu.SemaphoreType.DMA

    def vmem(*shape):
        return pltpu.VMEM(shape, jnp.float32)

    result = pl.pallas_call(
        kernel,
        out_shape=jax.ShapeDtypeStruct((PLANES, ROWS, LON), jnp.float32),
        in_specs=[hbm, pl.BlockSpec(memory_space=pltpu.SMEM), hbm, hbm],
        out_specs=pl.BlockSpec(memory_space=pltpu.VMEM),
        scratch_shapes=[
            pltpu.SMEM((2,), jnp.int32),
            vmem(PLANES, ROWS, LON),
            vmem(2 * NY, HALF // 2, ROWS, 128),
            vmem(NZ, 2, HALF // 2, ROWS, 128),
            vmem(2, HALF // 2, ROWS, 128),
            vmem(2, 2, HALF // 2, ROWS, 128),
            vmem(2, 2, HALF // 2, ROWS, 128),
            vmem(2 * NZ, ROWS, LON),
            vmem(NY, 2, ROWS, LON),
            vmem(2, ROWS, LON),
            vmem(2, 2, ROWS, LON),
            vmem(2, 2, ROWS, LON),
            vmem(*field),
            vmem(*field),
            vmem(*field),
            vmem(*field),
            dma((3, 2)),
            dma((3, 2)),
            dma((2, 2, 2)),
            dma((2, 2, 2, 2)),
            dma((2, 2, 2, 2)),
            dma((2, 2, 2)),
            dma((2, 2, 2)),
            dma((3,)),
        ],
        compiler_params=pltpu.CompilerParams(
            collective_id=0, has_side_effects=True, vmem_limit_bytes=32 * 2**20
        ),
        name="ensemble_adjoint",
    )(ckpt_index, seeds, slot, current)
    return result.reshape(1, 3, LEV, ROWS, LON)


def solution(mesh):
    return jax.shard_map(
        on_device,
        mesh=mesh,
        in_specs=(
            P("member", None, None, "band", None),
            P(),
            P(None, None, None, "band", None),
            P("member"),
        ),
        out_specs=P("member", None, None, "band", None),
        check_vma=False,
    )
```

time: 43.2 us -> 43.7 us (1.012)
  no operation moved by 1% of the time
where the time goes in v4:
time: 43.7 us; the launch traced here: 43.4 us
  Pallas kernels  42 us (96%)
  local copies, waits for them, and re-layouts  0.68 us (2%)
  between operations  0.66 us (2%)
    pallas_call x1, Pallas kernels, on_device(): pl.pallas_call(kernel, out_shape=jax.ShapeDtypeStruct((PLANES, ROWS, LON)...  42 us

profile of v4, /device:TPU:7, one launch (start us, length us, event | category | flops | bytes accessed | tf_op | source)
XLA Modules:
  0.0 43.4 jit_solution(9771717941597633517)
XLA Ops:
  0.7 42.0 %ensemble_adjoint.1 = f32[12,8,512]{2,1,0:T(8,128)S(1)} custom-call(s32[2]{0:T(128)} %index_hbm.1, s32[1]{0:T(128)S(6)} %copy.6.seed_ref, f32[12,8,512]{2,1,0:T(8,128)} %bitcast.5, f32[2,12,8,512]{3,2,1,0:T(8,128)} %bitcast.4), custom_call_target="tpu_custom_call" | custom-call | tf_op jit(solution)/shard_map/ensemble_adjoint/pallas_call | solution.py:475
  42.7 0.7 %copy.7 = f32[1,3,4,8,512]{4,3,2,1,0:T(8,128)} copy(f32[1,3,4,8,512]{4,3,2,1,0:T(8,128)S(1)} %bitcast.3) | data formatting | bytes 393216

commit v5 on v4

v5 whole, which is shorter than its diff:
```python
import functools

import jax
import jax.numpy as jnp
from jax import lax
from jax.experimental import pallas as pl
from jax.experimental.pallas import tpu as pltpu
from jax.sharding import PartitionSpec as P

NY = 8
NZ = 6
NBAND = 16
CHIPS = NBAND // 2
LEV = 4
PLANES = 3 * LEV
HALF = PLANES // 2
ROWS = 8
LON = 512
LAST_SLOT = NY * NZ - 1
EDGE = {1: 4, 0: 2}
P_CHUNKS, Q_CHUNKS = HALF // 2, 4
WIDTH = LON // Q_CHUNKS
MESH = pl.DeviceIdType.MESH


def next_lon(x):
    return pltpu.roll(x, LON - 1, 1)


def prev_lon(x):
    return pltpu.roll(x, 1, 1)


def next_row(x):
    return pltpu.roll(x, 2 * ROWS - 1, 0)


def prev_row(x):
    return pltpu.roll(x, 1, 0)


def advance(east, north, height):
    diff_east = 0.1 * (next_lon(east) - prev_lon(east))
    diff_north = 0.1 * (next_lon(north) - prev_lon(north))
    diff_height = 0.1 * (next_lon(height) - prev_lon(height))
    return (
        east - (east * diff_east + diff_height),
        north - east * diff_north,
        height - (east * diff_height + diff_east),
    )


def coefficients(state):
    east, north, height = state
    depth = 0.1 * jnp.exp(0.25 * height)
    visc = 0.04 + 0.02 * jnp.tanh(height)
    east, north = 0.1 * east, 0.1 * north
    return depth, 1.0 - 4.0 * visc, visc + east, visc - east, visc + north, visc - north


def adjoint_step(factors, adjoint, keep):
    depth, middle, c_next, c_prev, r_next, r_prev = factors
    a, b, c = adjoint

    def spread(f, zonal=None, merid=None):
        if zonal is None:
            zonal = merid = 0.0
        return (
            middle * f
            + next_lon(c_next * f + zonal)
            + prev_lon(c_prev * f - zonal)
            + next_row(r_next * f + merid)
            + prev_row(r_prev * f - merid)
        )

    new_a = spread(a) + depth * (next_lon(c) - prev_lon(c))
    new_b = spread(b) + depth * (next_row(c) - prev_row(c))
    new_c = spread(c, 0.1 * a, 0.1 * b)
    return tuple(jnp.where(keep, f, 0.0) for f in (new_a, new_b, new_c))


def kernel(
    index_hbm, seed_ref, ckpt, innov, out,
    index_ref, slot,
    p_meter, p_rows_in, p_cols_in, p_last, p_mine, p_edge,
    q_meter, q_cols_in, q_rows_in, q_last, q_mine, q_edge,
    own, edge, force, force_edge, factor,
    p_sem, q_sem, gather_sem, cross_sem, spread_sem, edge_sem, force_sem, local_sem, ready_sem,
):
    band = lax.axis_index("band")
    member = lax.axis_index("member")
    y, z = lax.rem(member, NY), member // NY
    chip = band // 2
    odd = lax.rem(band, 2) == 1
    even = jnp.logical_not(odd)
    has_up, has_down = band < NBAND - 1, band > 0
    chip_up = chip < CHIPS - 1
    far_up, far_down = chip == CHIPS // 2 - 1, chip == CHIPS // 2
    near_up = jnp.logical_and(has_up, band != CHIPS - 1)
    near_down = jnp.logical_and(has_down, band != CHIPS)
    z_above = jnp.where(far_up, NZ - 1 - z, z)
    z_below = jnp.where(far_down, NZ - 1 - z, z)
    member_up = z_above * NY + y
    member_down = z_below * NY + y

    y_peers = [lax.rem(y + step, NY) for step in range(1, NY)]
    z_peers = [lax.rem(z + step, NZ) for step in range(1, NZ)]
    low_band, high_band = 2 * chip, 2 * chip + 1

    def at_y(peer, of_band):
        return {"band": of_band, "member": z * NY + peer}

    def at_z(peer, of_band):
        return {"band": of_band, "member": peer * NY + y}

    sibling = {"band": low_band + high_band - band}
    up = {"band": band + 1, "member": jnp.where(odd, member_up, member)}
    down = {"band": band - 1, "member": jnp.where(odd, member, member_down)}
    handler_up = {"band": band + 2, "member": member_up}
    handler_down = {"band": band - 2, "member": member_down}

    def low_rows(k):
        return slice(0, EDGE[k])

    def high_rows(k):
        return slice(ROWS - EDGE[k], ROWS)

    def p_part(peer, rows=slice(None)):
        planes = pl.ds((HALF // 2) * (peer // 4), HALF // 2)
        return planes, rows, pl.ds(pl.multiple_of(128 * lax.rem(peer, 4), 128), 128)

    def q_part(peer, rows=slice(None)):
        return HALF + peer, rows

    def p_chunk(peer, i):
        lanes = pl.ds(pl.multiple_of(128 * lax.rem(peer, 4), 128), 128)
        return P_CHUNKS * (peer // 4) + i, slice(None), lanes

    def q_lanes(i):
        return slice(WIDTH * i, WIDTH * (i + 1))

    def q_chunk(peer, i):
        return HALF + peer, slice(None), q_lanes(i)

    def send(src, dst, sems, device):
        return pltpu.make_async_remote_copy(
            src_ref=src, dst_ref=dst, send_sem=sems.at[0], recv_sem=sems.at[1],
            device_id=device, device_id_type=MESH,
        )

    def drain(ref, sems):
        return send(ref, ref, sems, sibling)

    def p_pieces(count, rows=slice(None)):
        return p_meter.at[:, pl.ds(0, count), rows]

    def q_planes(count, rows=slice(None)):
        return q_meter.at[:, pl.ds(0, count), rows]

    def copy(src, dst, number):
        return pltpu.make_async_copy(src, dst, local_sem.at[number])

    barrier = pltpu.get_barrier_semaphore()

    def greet(device):
        pl.semaphore_signal(barrier, inc=1, device_id=device, device_id_type=MESH)

    for peer in z_peers:
        greet(at_z(peer, high_band))
    for peer in y_peers:
        greet(at_y(peer, high_band))
    greet(sibling)

    @pl.when(odd)
    def _():
        for peer in z_peers:
            greet(at_z(peer, low_band))
        for peer in y_peers:
            greet(at_y(peer, low_band))
        pl.when(chip_up)(lambda: greet(up))
        pl.when(far_up)(lambda: greet(handler_up))

    pl.when(jnp.logical_and(even, near_down))(lambda: greet(down))

    load_slot = copy(ckpt, slot, 0)
    load_index = copy(index_hbm, index_ref, 1)
    load_force = copy(innov, force, 2)
    load_slot.start()
    load_index.start()
    load_force.start()
    load_slot.wait()
    peers = NY + NZ - 2
    alone = jnp.logical_or(far_up, chip == CHIPS - 1)
    plain = jnp.logical_not(jnp.logical_or(alone, far_down))
    for condition, count in (
        (band == 0, peers + 1),
        (jnp.logical_and(even, has_down), peers + 2),
        (jnp.logical_and(odd, alone), 2 * peers + 1),
        (jnp.logical_and(odd, plain), 2 * peers + 2),
        (jnp.logical_and(odd, far_down), 2 * peers + 3),
    ):
        pl.when(condition)(functools.partial(pl.semaphore_wait, barrier, count))

    def tell(number, device):
        pl.semaphore_signal(ready_sem.at[number], inc=1, device_id=device, device_id_type=MESH)

    pl.when(jnp.logical_and(even, far_down))(lambda: tell(0, down))
    pl.when(jnp.logical_and(odd, far_down))(lambda: tell(1, handler_down))

    def spots(core):
        return core * NZ + z, core * NY + y

    streams = [("q", 0), ("p", 0), ("q", 1), ("p", 1), ("q", 2), ("p", 2), ("q", 3)]

    def first_phase(core):
        q_spot, p_spot = spots(core)
        for kind, i in streams:
            if kind == "p":
                for peer in y_peers:
                    send(slot.at[p_chunk(peer, i)], p_rows_in[i].at[p_spot], p_sem.at[0, i], at_y(peer, high_band)).start()
                if core == 0:
                    send(slot.at[p_chunk(y, i)], p_rows_in[i].at[p_spot], p_sem.at[0, i], sibling).start()
                else:
                    p_rows_in[i][p_spot] = slot[p_chunk(y, i)]
            else:
                for peer in z_peers:
                    send(slot.at[q_chunk(peer, i)], q_cols_in[i].at[q_spot], q_sem.at[0, i], at_z(peer, high_band)).start()
                if core == 0:
                    send(slot.at[q_chunk(z, i)], q_cols_in[i].at[q_spot], q_sem.at[0, i], sibling).start()
                else:
                    q_cols_in[i][q_spot] = slot[q_chunk(z, i)]

    pl.when(even)(lambda: first_phase(0))
    pl.when(odd)(lambda: first_phase(1))

    everything, p_planes, q_planes_all = slice(0, PLANES), slice(0, HALF), slice(HALF, PLANES)

    def edge_up(src, dst, sems, k, planes, device):
        rows = (k, planes, high_rows(k))
        return send(src.at[rows], dst.at[rows], sems.at[k, 0], device)

    def edge_down(src, dst, sems, k, planes, device):
        rows = (k, planes, low_rows(k))
        return send(src.at[rows], dst.at[rows], sems.at[k, 1], device)

    def start_edges(src, dst, sems, k, planes, upward, downward):
        pl.when(upward)(lambda: edge_up(src, dst, sems, k, planes, up).start())
        pl.when(downward)(lambda: edge_down(src, dst, sems, k, planes, down).start())

    def finish_edges(src, dst, sems, k, planes, upward, downward):
        def upper():
            edge_up(src, dst, sems, k, planes, up).wait_send()
            edge_down(src, dst, sems, k, planes, up).wait_recv()

        def lower():
            edge_down(src, dst, sems, k, planes, down).wait_send()
            edge_up(src, dst, sems, k, planes, down).wait_recv()

        pl.when(upward)(upper)
        pl.when(downward)(lower)

    for k in (1, 0):
        start_edges(innov, force_edge, force_sem, k, everything, near_up, has_down)

    load_index.wait()
    seed = seed_ref[0]
    index = [index_ref[0], index_ref[1]]
    other = jnp.where(index[0] == LAST_SLOT, index[1], index[0])
    other_y, other_z = lax.rem(other, NY), other // NY
    load_force.wait()
    for k in range(2):
        for plane in range(PLANES):
            force[k, plane] = pltpu.roll(force[k, plane], seed, 1)

    @pl.when(odd)
    def _():
        for kind, i in streams:
            if kind == "p":
                drain(p_rows_in[i].at[pl.ds(0, 2 * NY - 1)], p_sem.at[0, i]).wait_recv()
                for core in range(2):
                    p_cols_in[i][z, core] = p_rows_in[i][core * NY + other_y]
                for peer in z_peers:
                    send(p_cols_in[i].at[z], p_cols_in[i].at[z], p_sem.at[1, i], at_z(peer, high_band)).start()

                @pl.when(z == NZ - 1)
                def _():
                    for core in range(2):
                        p_last[i, core] = p_rows_in[i][core * NY + NY - 1]
                    for peer in z_peers:
                        send(p_last.at[i], p_last.at[i], p_sem.at[2, i], at_z(peer, high_band)).start()
            else:
                drain(q_cols_in[i].at[pl.ds(0, 2 * NZ - 1)], q_sem.at[0, i]).wait_recv()
                for core in range(2):
                    q_rows_in[i][y, core] = q_cols_in[i][core * NZ + other_z]
                for peer in y_peers:
                    send(q_rows_in[i].at[y], q_rows_in[i].at[y], q_sem.at[1, i], at_y(peer, high_band)).start()

                @pl.when(y == NY - 1)
                def _():
                    for core in range(2):
                        q_last[i, core] = q_cols_in[i][core * NZ + NZ - 1]
                    for peer in y_peers:
                        send(q_last.at[i], q_last.at[i], q_sem.at[2, i], at_y(peer, high_band)).start()

        def cross_up(mine, landing, kind, k, rows):
            return send(
                mine.at[(k, 1) + rows(high_rows(k))], landing.at[(1, k) + rows(high_rows(k))],
                cross_sem.at[0, kind, k], handler_up,
            )

        def cross_down(mine, landing, kind, k, rows):
            return send(
                mine.at[(k, 0) + rows(low_rows(k))], landing.at[(0, k) + rows(low_rows(k))],
                cross_sem.at[1, kind, k], handler_down,
            )

        def p_rows(rows):
            return slice(None), rows

        def q_rows(rows):
            return (rows,)

        def start_cross(*job):
            pl.when(far_up)(lambda: cross_up(*job).start())
            pl.when(far_down)(lambda: cross_down(*job).start())

        for kind, i in streams:
            if kind == "p":
                drain(p_cols_in[i].at[pl.ds(0, NZ - 1)], p_sem.at[1, i]).wait()
                pl.when(z == NZ - 1)(lambda: drain(p_cols_in[i].at[pl.ds(0, NZ - 1)], p_sem.at[2, i]).wait_send())
                pl.when(z < NZ - 1)(lambda: drain(p_last.at[i], p_sem.at[2, i]).wait_recv())
                from_other, from_last = p_cols_in[i][other_z], p_last[i]
                for k in (1, 0):
                    p_mine[k, :, i] = jnp.where(index[k] == LAST_SLOT, from_last, from_other)
                place = (slice(None),) + p_chunk(y, i)
                send(p_mine.at[:, 0, i], own.at[place], gather_sem.at[0, 0], sibling).start()
                for peer in y_peers:
                    send(p_mine.at[:, 0, i], own.at[place], gather_sem.at[0, 0], at_y(peer, low_band)).start()
                    send(p_mine.at[:, 1, i], own.at[place], gather_sem.at[1, 0], at_y(peer, high_band)).start()
                if i == P_CHUNKS - 1:
                    @pl.when(far_up)
                    def _():
                        pl.semaphore_wait(ready_sem.at[0], 1)
                        pl.semaphore_wait(ready_sem.at[1], 1)
                        for k in (1, 0):
                            edge_up(innov, force_edge, force_sem, k, everything, up).start()

                for k in (1, 0):
                    own[(k,) + p_chunk(y, i)] = p_mine[k, 1, i]
                    if i == P_CHUNKS - 1:
                        start_cross(p_mine, p_edge, 0, k, p_rows)
            else:
                drain(q_rows_in[i].at[pl.ds(0, NY - 1)], q_sem.at[1, i]).wait()
                pl.when(y == NY - 1)(lambda: drain(q_rows_in[i].at[pl.ds(0, NY - 1)], q_sem.at[2, i]).wait_send())
                pl.when(y < NY - 1)(lambda: drain(q_last.at[i], q_sem.at[2, i]).wait_recv())
                from_other, from_last = q_rows_in[i][other_y], q_last[i]
                for k in (1, 0):
                    q_mine[k, :, :, q_lanes(i)] = jnp.where(index[k] == LAST_SLOT, from_last, from_other)
                place = (slice(None),) + q_chunk(z, i)
                send(q_mine.at[:, 0, :, q_lanes(i)], own.at[place], gather_sem.at[0, 1], sibling).start()
                for peer in z_peers:
                    send(q_mine.at[:, 0, :, q_lanes(i)], own.at[place], gather_sem.at[0, 1], at_z(peer, low_band)).start()
                    send(q_mine.at[:, 1, :, q_lanes(i)], own.at[place], gather_sem.at[1, 1], at_z(peer, high_band)).start()
                for k in (1, 0):
                    own[(k,) + q_chunk(z, i)] = q_mine[k, 1, :, q_lanes(i)]
                    if i == Q_CHUNKS - 1:
                        start_cross(q_mine, q_edge, 1, k, q_rows)

        def spread_p(k):
            @pl.when(far_down)
            def _():
                cross_up(p_mine, p_edge, 0, k, p_rows).wait_recv()
                piece, place = p_edge.at[1, k, :, high_rows(k)], (k,) + p_part(y, high_rows(k))
                send(piece, edge.at[place], spread_sem.at[0, k, 0], sibling).start()
                for peer in y_peers:
                    send(piece, edge.at[place], spread_sem.at[0, k, 0], at_y(peer, low_band)).start()

            @pl.when(far_up)
            def _():
                cross_down(p_mine, p_edge, 0, k, p_rows).wait_recv()
                piece, place = p_edge.at[0, k, :, low_rows(k)], (k,) + p_part(y, low_rows(k))
                for peer in y_peers:
                    send(piece, edge.at[place], spread_sem.at[1, k, 0], at_y(peer, high_band)).start()
                edge[place] = p_edge[0, k, :, low_rows(k)]

        def spread_q(k):
            @pl.when(far_down)
            def _():
                cross_up(q_mine, q_edge, 1, k, q_rows).wait_recv()
                piece, place = q_edge.at[1, k, high_rows(k)], (k,) + q_part(z_below, high_rows(k))
                send(piece, edge.at[place], spread_sem.at[0, k, 1], sibling).start()
                for peer in z_peers:
                    send(piece, edge.at[place], spread_sem.at[0, k, 1], at_z(peer, low_band)).start()

            @pl.when(far_up)
            def _():
                cross_down(q_mine, q_edge, 1, k, q_rows).wait_recv()
                piece, place = q_edge.at[0, k, low_rows(k)], (k,) + q_part(z_above, low_rows(k))
                for peer in z_peers:
                    send(piece, edge.at[place], spread_sem.at[1, k, 1], at_z(peer, high_band)).start()
                edge[place] = q_edge[0, k, low_rows(k)]

        for k in (1, 0):
            spread_p(k)
        for k in (1, 0):
            spread_q(k)

    def gathered(part, pieces, planes):
        pl.when(odd)(lambda: drain(pieces[0], gather_sem.at[1, part]).wait_recv())
        pl.when(even)(lambda: drain(pieces[1], gather_sem.at[0, part]).wait_recv())
        for k in (1, 0):
            start_edges(own, edge, edge_sem.at[part], k, planes, near_up, near_down)

    def factors_of(state):
        return coefficients(advance(*state)), coefficients(state)

    gathered(0, (p_pieces(2 * NY - 2), p_pieces(2 * NY)), p_planes)
    gathered(1, (q_planes(2 * NZ - 2), q_planes(2 * NZ)), q_planes_all)

    row = lax.broadcasted_iota(jnp.int32, (ROWS, LON), 0)
    inside = jnp.logical_not(
        jnp.logical_or(
            jnp.logical_and(band == NBAND - 1, row < ROWS // 2),
            jnp.logical_and(band == 0, row >= ROWS // 2),
        )
    )
    keep = jnp.logical_or(
        lax.broadcasted_iota(jnp.int32, (2 * ROWS, LON), 0) < ROWS,
        jnp.concatenate([inside, inside], axis=0),
    )

    for k in (1, 0):
        finish_edges(innov, force_edge, force_sem, k, everything, has_up, has_down)
        for plane in range(PLANES):
            force_edge[k, plane] = pltpu.roll(force_edge[k, plane], seed, 1)

    for k in (1, 0):
        for lev in range(LEV):
            state = tuple(own[k, comp * LEV + lev] for comp in range(3))
            for step, values in enumerate(factors_of(state)):
                for number, value in enumerate(values):
                    factor[k, lev, step, number] = value

    adjoint = [None] * LEV
    for k in (1, 0):
        @pl.when(jnp.logical_and(even, far_down))
        def _():
            drain(p_pieces(NY, high_rows(k)), spread_sem.at[0, k, 0]).wait_recv()
            drain(q_planes(NZ, high_rows(k)), spread_sem.at[0, k, 1]).wait_recv()

        @pl.when(jnp.logical_and(odd, far_up))
        def _():
            drain(p_pieces(NY - 1, low_rows(k)), spread_sem.at[1, k, 0]).wait_recv()
            drain(q_planes(NZ - 1, low_rows(k)), spread_sem.at[1, k, 1]).wait_recv()

        finish_edges(own, edge, edge_sem.at[0], k, p_planes, near_up, near_down)
        finish_edges(own, edge, edge_sem.at[1], k, q_planes_all, near_up, near_down)
        for lev in range(LEV):
            def both(inner_ref, outer_ref):
                return tuple(
                    jnp.concatenate(
                        [
                            inner_ref[k, comp * LEV + lev],
                            jnp.where(inside, outer_ref[k, comp * LEV + lev], 0.0),
                        ],
                        axis=0,
                    )
                    for comp in range(3)
                )

            forcing = both(force, force_edge)
            if adjoint[lev] is None:
                field = forcing
            else:
                field = tuple(f + g for f, g in zip(adjoint[lev], forcing))
            outer = tuple(jnp.where(inside, edge[k, comp * LEV + lev], 0.0) for comp in range(3))
            for step, values in enumerate(factors_of(outer)):
                whole = tuple(
                    jnp.concatenate([factor[k, lev, step, number], value], axis=0)
                    for number, value in enumerate(values)
                )
                field = adjoint_step(whole, field, keep)
            if k == 1:
                adjoint[lev] = field
            else:
                for comp in range(3):
                    out[comp * LEV + lev] = field[comp][:ROWS]

    def first_left(p_count, q_count):
        for i in range(P_CHUNKS):
            drain(p_rows_in[i].at[pl.ds(0, p_count)], p_sem.at[0, i]).wait_send()
        for i in range(Q_CHUNKS):
            drain(q_cols_in[i].at[pl.ds(0, q_count)], q_sem.at[0, i]).wait_send()

    pl.when(even)(lambda: first_left(NY, NZ))

    @pl.when(odd)
    def _():
        first_left(NY - 1, NZ - 1)
        drain(p_pieces(2 * NY), gather_sem.at[0, 0]).wait_send()
        drain(p_pieces(2 * NY - 2), gather_sem.at[1, 0]).wait_send()
        drain(q_planes(2 * NZ), gather_sem.at[0, 1]).wait_send()
        drain(q_planes(2 * NZ - 2), gather_sem.at[1, 1]).wait_send()
        for k in (1, 0):
            @pl.when(far_up)
            def _():
                drain(p_edge.at[0, k, :, high_rows(k)], cross_sem.at[0, 0, k]).wait_send()
                drain(q_edge.at[0, k, high_rows(k)], cross_sem.at[0, 1, k]).wait_send()
                drain(p_pieces(NY - 1, low_rows(k)), spread_sem.at[1, k, 0]).wait_send()
                drain(q_planes(NZ - 1, low_rows(k)), spread_sem.at[1, k, 1]).wait_send()

            @pl.when(far_down)
            def _():
                drain(p_edge.at[0, k, :, low_rows(k)], cross_sem.at[1, 0, k]).wait_send()
                drain(q_edge.at[0, k, low_rows(k)], cross_sem.at[1, 1, k]).wait_send()
                drain(p_pieces(NY, high_rows(k)), spread_sem.at[0, k, 0]).wait_send()
                drain(q_planes(NZ, high_rows(k)), spread_sem.at[0, k, 1]).wait_send()


def on_device(checkpoints, ckpt_index, innovations, seeds):
    slot = checkpoints.reshape(PLANES, ROWS, LON)
    current = innovations.reshape(2, PLANES, ROWS, LON)
    hbm = pl.BlockSpec(memory_space=pltpu.HBM)
    slot, current, ckpt_index = (
        pltpu.with_memory_space_constraint(operand, pltpu.HBM) for operand in (slot, current, ckpt_index)
    )
    field = (2, PLANES, ROWS, LON)
    dma = pltpu.SemaphoreType.DMA

    def vmem(*shape):
        return pltpu.VMEM(shape, jnp.float32)

    result = pl.pallas_call(
        kernel,
        out_shape=jax.ShapeDtypeStruct((PLANES, ROWS, LON), jnp.float32),
        in_specs=[hbm, pl.BlockSpec(memory_space=pltpu.SMEM), hbm, hbm],
        out_specs=pl.BlockSpec(memory_space=pltpu.VMEM),
        scratch_shapes=[
            pltpu.SMEM((2,), jnp.int32),
            vmem(PLANES, ROWS, LON),
            vmem(P_CHUNKS, 2 * NY, ROWS, 128),
            [vmem(2 * NY, ROWS, 128)] * P_CHUNKS,
            [vmem(NZ, 2, ROWS, 128)] * P_CHUNKS,
            vmem(P_CHUNKS, 2, ROWS, 128),
            vmem(2, 2, P_CHUNKS, ROWS, 128),
            vmem(2, 2, P_CHUNKS, ROWS, 128),
            vmem(Q_CHUNKS, 2 * NZ, ROWS, WIDTH),
            [vmem(2 * NZ, ROWS, WIDTH)] * Q_CHUNKS,
            [vmem(NY, 2, ROWS, WIDTH)] * Q_CHUNKS,
            vmem(Q_CHUNKS, 2, ROWS, WIDTH),
            vmem(2, 2, ROWS, LON),
            vmem(2, 2, ROWS, LON),
            vmem(*field),
            vmem(*field),
            vmem(*field),
            vmem(*field),
            vmem(2, LEV, 2, 6, ROWS, LON),
            dma((3, P_CHUNKS, 2)),
            dma((3, Q_CHUNKS, 2)),
            dma((2, 2, 2)),
            dma((2, 2, 2, 2)),
            dma((2, 2, 2, 2)),
            dma((2, 2, 2, 2)),
            dma((2, 2, 2)),
            dma((3,)),
            pltpu.SemaphoreType.REGULAR((2,)),
        ],
        compiler_params=pltpu.CompilerParams(
            collective_id=0, has_side_effects=True, vmem_limit_bytes=32 * 2**20
        ),
        name="ensemble_adjoint",
    )(ckpt_index, seeds, slot, current)
    return result.reshape(1, 3, LEV, ROWS, LON)


def solution(mesh):
    return jax.shard_map(
        on_device,
        mesh=mesh,
        in_specs=(
            P("member", None, None, "band", None),
            P(),
            P(None, None, None, "band", None),
            P("member"),
        ),
        out_specs=P("member", None, None, "band", None),
        check_vma=False,
    )
```

time: 43.7 us -> 41.9 us (0.959)
  Pallas kernels: 42 us -> 40.4 us
    pallas_call x1, Pallas kernels: 42 us -> 40.4 us  [on_device(): pl.pallas_call(kernel, out_shape=jax.ShapeDtypeStruct((PLANES, ROWS, LON)...]
where the time goes in v5:
time: 41.9 us; the launch traced here: 41.8 us
  Pallas kernels  40.4 us (96%)
  local copies, waits for them, and re-layouts  0.68 us (2%)
  between operations  0.66 us (2%)
    pallas_call x1, Pallas kernels, on_device(): pl.pallas_call(kernel, out_shape=jax.ShapeDtypeStruct((PLANES, ROWS, LON)...  40.4 us

profile of v5, /device:TPU:7, one launch (start us, length us, event | category | flops | bytes accessed | tf_op | source)
XLA Modules:
  0.0 41.8 jit_solution(1281687706344174586)
XLA Ops:
  0.7 40.4 %ensemble_adjoint.1 = f32[12,8,512]{2,1,0:T(8,128)S(1)} custom-call(s32[2]{0:T(128)} %index_hbm.1, s32[1]{0:T(128)S(6)} %copy.6.seed_ref, f32[12,8,512]{2,1,0:T(8,128)} %bitcast.5, f32[2,12,8,512]{3,2,1,0:T(8,128)} %bitcast.4), custom_call_target="tpu_custom_call" | custom-call | tf_op jit(solution)/shard_map/ensemble_adjoint/pallas_call | solution.py:533
  41.1 0.7 %copy.7 = f32[1,3,4,8,512]{4,3,2,1,0:T(8,128)} copy(f32[1,3,4,8,512]{4,3,2,1,0:T(8,128)S(1)} %bitcast.3) | data formatting | bytes 393216

commit v6 on v5

--- a/solution.py
+++ b/solution.py
@@ -103,7 +103,7 @@
     member_up = z_above * NY + y
     member_down = z_below * NY + y
 
-    y_peers = [lax.rem(y + step, NY) for step in range(1, NY)]
+    y_peers = [lax.rem(y + step, NY) for step in (4, 3, 5, 2, 6, 1, 7)]
     z_peers = [lax.rem(z + step, NZ) for step in range(1, NZ)]
     low_band, high_band = 2 * chip, 2 * chip + 1
 

time: 41.9 us -> 42 us (level)
  no operation moved by 1% of the time
where the time goes in v6:
time: 42 us; the launch traced here: 41.9 us
  Pallas kernels  40.5 us (96%)
  local copies, waits for them, and re-layouts  0.68 us (2%)
  between operations  0.66 us (2%)
    pallas_call x1, Pallas kernels, on_device(): pl.pallas_call(kernel, out_shape=jax.ShapeDtypeStruct((PLANES, ROWS, LON)...  40.5 us

profile of v6, /device:TPU:7, one launch (start us, length us, event | category | flops | bytes accessed | tf_op | source)
XLA Modules:
  0.0 41.9 jit_solution(17965114593609758991)
XLA Ops:
  0.7 40.5 %ensemble_adjoint.1 = f32[12,8,512]{2,1,0:T(8,128)S(1)} custom-call(s32[2]{0:T(128)} %index_hbm.1, s32[1]{0:T(128)S(6)} %copy.6.seed_ref, f32[12,8,512]{2,1,0:T(8,128)} %bitcast.5, f32[2,12,8,512]{3,2,1,0:T(8,128)} %bitcast.4), custom_call_target="tpu_custom_call" | custom-call | tf_op jit(solution)/shard_map/ensemble_adjoint/pallas_call | solution.py:533
  41.2 0.7 %copy.7 = f32[1,3,4,8,512]{4,3,2,1,0:T(8,128)} copy(f32[1,3,4,8,512]{4,3,2,1,0:T(8,128)S(1)} %bitcast.3) | data formatting | bytes 393216

commit v7 on v6

--- a/solution.py
+++ b/solution.py
@@ -104,7 +104,7 @@
     member_down = z_below * NY + y
 
     y_peers = [lax.rem(y + step, NY) for step in (4, 3, 5, 2, 6, 1, 7)]
-    z_peers = [lax.rem(z + step, NZ) for step in range(1, NZ)]
+    z_peers = [lax.rem(z + jnp.where(z < NZ // 2, NZ - step, step), NZ) for step in range(1, NZ)]
     low_band, high_band = 2 * chip, 2 * chip + 1
 
     def at_y(peer, of_band):
@@ -332,11 +332,6 @@
                 from_other, from_last = p_cols_in[i][other_z], p_last[i]
                 for k in (1, 0):
                     p_mine[k, :, i] = jnp.where(index[k] == LAST_SLOT, from_last, from_other)
-                place = (slice(None),) + p_chunk(y, i)
-                send(p_mine.at[:, 0, i], own.at[place], gather_sem.at[0, 0], sibling).start()
-                for peer in y_peers:
-                    send(p_mine.at[:, 0, i], own.at[place], gather_sem.at[0, 0], at_y(peer, low_band)).start()
-                    send(p_mine.at[:, 1, i], own.at[place], gather_sem.at[1, 0], at_y(peer, high_band)).start()
                 if i == P_CHUNKS - 1:
                     @pl.when(far_up)
                     def _():
@@ -344,11 +339,16 @@
                         pl.semaphore_wait(ready_sem.at[1], 1)
                         for k in (1, 0):
                             edge_up(innov, force_edge, force_sem, k, everything, up).start()
-
+                if i == P_CHUNKS - 1:
+                    for k in (1, 0):
+                        start_cross(p_mine, p_edge, 0, k, p_rows)
+                place = (slice(None),) + p_chunk(y, i)
+                send(p_mine.at[:, 0, i], own.at[place], gather_sem.at[0, 0], sibling).start()
+                for peer in y_peers:
+                    send(p_mine.at[:, 0, i], own.at[place], gather_sem.at[0, 0], at_y(peer, low_band)).start()
+                    send(p_mine.at[:, 1, i], own.at[place], gather_sem.at[1, 0], at_y(peer, high_band)).start()
                 for k in (1, 0):
                     own[(k,) + p_chunk(y, i)] = p_mine[k, 1, i]
-                    if i == P_CHUNKS - 1:
-                        start_cross(p_mine, p_edge, 0, k, p_rows)
             else:
                 drain(q_rows_in[i].at[pl.ds(0, NY - 1)], q_sem.at[1, i]).wait()
                 pl.when(y == NY - 1)(lambda: drain(q_rows_in[i].at[pl.ds(0, NY - 1)], q_sem.at[2, i]).wait_send())
@@ -356,6 +356,9 @@
                 from_other, from_last = q_rows_in[i][other_y], q_last[i]
                 for k in (1, 0):
                     q_mine[k, :, :, q_lanes(i)] = jnp.where(index[k] == LAST_SLOT, from_last, from_other)
+                if i == Q_CHUNKS - 1:
+                    for k in (1, 0):
+                        start_cross(q_mine, q_edge, 1, k, q_rows)
                 place = (slice(None),) + q_chunk(z, i)
                 send(q_mine.at[:, 0, :, q_lanes(i)], own.at[place], gather_sem.at[0, 1], sibling).start()
                 for peer in z_peers:
@@ -363,8 +366,6 @@
                     send(q_mine.at[:, 1, :, q_lanes(i)], own.at[place], gather_sem.at[1, 1], at_z(peer, high_band)).start()
                 for k in (1, 0):
                     own[(k,) + q_chunk(z, i)] = q_mine[k, 1, :, q_lanes(i)]
-                    if i == Q_CHUNKS - 1:
-                        start_cross(q_mine, q_edge, 1, k, q_rows)
 
         def spread_p(k):
             @pl.when(far_down)

time: 42 us -> 41.3 us (0.983)
  Pallas kernels: 40.5 us -> 39.8 us
    pallas_call x1, Pallas kernels: 40.5 us -> 39.8 us  [on_device(): pl.pallas_call(kernel, out_shape=jax.ShapeDtypeStruct((PLANES, ROWS, LON)...]
where the time goes in v7:
time: 41.3 us; the launch traced here: 41.2 us
  Pallas kernels  39.8 us (96%)
  local copies, waits for them, and re-layouts  0.68 us (2%)
  between operations  0.66 us (2%)
    pallas_call x1, Pallas kernels, on_device(): pl.pallas_call(kernel, out_shape=jax.ShapeDtypeStruct((PLANES, ROWS, LON)...  39.8 us

profile of v7, /device:TPU:7, one launch (start us, length us, event | category | flops | bytes accessed | tf_op | source)
XLA Modules:
  0.0 41.2 jit_solution(4701180864094265569)
XLA Ops:
  0.7 39.8 %ensemble_adjoint.1 = f32[12,8,512]{2,1,0:T(8,128)S(1)} custom-call(s32[2]{0:T(128)} %index_hbm.1, s32[1]{0:T(128)S(6)} %copy.6.seed_ref, f32[12,8,512]{2,1,0:T(8,128)} %bitcast.5, f32[2,12,8,512]{3,2,1,0:T(8,128)} %bitcast.4), custom_call_target="tpu_custom_call" | custom-call | tf_op jit(solution)/shard_map/ensemble_adjoint/pallas_call | solution.py:534
  40.5 0.7 %copy.7 = f32[1,3,4,8,512]{4,3,2,1,0:T(8,128)} copy(f32[1,3,4,8,512]{4,3,2,1,0:T(8,128)S(1)} %bitcast.3) | data formatting | bytes 393216
